TPU v7x, 256 devices: a whole 4x4x8 slice. The times are simulated.
256 devices in a mesh: dom: 16 (over z, core), mem: 16 (over y, x).
Axes of the slice: x: 4, y: 4, z: 8, core: 2. Of those that a mesh axis runs over, the one named last changes fastest.
Arguments:
- coarse_latents: bfloat16 [16, 8192, 512], P('mem', 'dom'), may hold values from -6 to 6
- send_rows: int32 [16, 16, 128], P('dom'), may hold values from 0 to 511
- up_index: int32 [3, 32768], P(None, 'dom'), may hold values from 0 to 2047
- up_weight: float32 [3, 32768], P(None, 'dom'), may hold values from 0.2 to 1
- neighbors: int32 [6, 32768], P(None, 'dom'), may hold values from 0 to 2303, as said below
- live_counts: int32 [16], P('dom'), may hold values from 1 to 2048, 24576 in all
- area: float32 [32768], P('dom'), may hold values from 0.25 to 4.5
- fine_skip: bfloat16 [32768, 512], P('dom'), may hold values from -6 to 6
- targets: bfloat16 [83, 32768], P(None, 'dom'), may hold values from -6 to 6
- kernel_width: float32 [83], replicated, may hold values from 0.5 to 2
- w_in: bfloat16 [1024, 512], replicated, may hold values from -0.1875 to 0.1875
- w_out: bfloat16 [512, 512], replicated, may hold values from -0.25 to 0.25
- ln_gain: float32 [512], replicated, may hold values from 0.1 to 1.9
- w_head: bfloat16 [512, 83], replicated, may hold values from -0.25 to 0.25
Outputs:
- grad_latent: bfloat16 [16, 32768, 512], P('mem', 'dom')
- grad_head: float32 [16, 512, 83], P('dom')
Inputs may be any that keep to these rules, and one draw needn't show every extreme that they name: neighbors[k, p] = 128 + (p % 2048) + e with -128 <= e <= 128.
All inputs are finite; a program needn't handle non-finite values. No bound on the sum of `live_counts` on one device may be relied on, other than what follows from the above.
Results may differ from a plain program's by a relative error of at most 0.015.
The roundings to bfloat16 on the way count: a program that leaves them out, or rounds other values in their place, can miss the bound.
Values may be sent and summed in bfloat16 or wider, within the bound.
A program may use at most 128 MiB of HBM per device.

v0:
```python
import math

import jax
import jax.numpy as jnp
from jax import lax
from jax.sharding import Mesh
from jax.sharding import PartitionSpec as P

K_NB = 6
RIM = 128
MEM = ("mem_0", "mem_1")


def extended_2(value, sides, width):
    for axis, dim in sides:
        count, length = (lax.axis_size(axis), value.shape[dim])
        up = [(i, (i + 1) % count) for i in range(count - 1)]
        down = [(j, i) for i, j in up]
        last = lax.slice_in_dim(value, length - width, length, axis=dim)
        first = lax.slice_in_dim(value, 0, width, axis=dim)
        before = lax.ppermute(last, axis, up)
        after = lax.ppermute(first, axis, down)
        value = jnp.concatenate([before, value, after], axis=dim)
    return value


def cut_along(value, dim, count):
    before, after = (value.shape[:dim], value.shape[dim + 1 :])
    return jnp.moveaxis(value.reshape(*before, count, -1, *after), dim, 0)


def laid_out(tiles, dim):
    lengths = list(tiles.shape[1:])
    lengths[dim] *= tiles.shape[0]
    return jnp.moveaxis(tiles, 0, dim).reshape(lengths)


def turned_blocks(tiles, axes, turns):
    lengths = [lax.axis_size(a) for a in axes]
    tiles = tiles.reshape(*lengths, *tiles.shape[1:])
    for k in turns:
        tiles = lax.all_to_all(tiles, axes[k], split_axis=k, concat_axis=k, tiled=True)
    return tiles.reshape(-1, *tiles.shape[len(axes) :])


def one_axis_at_a_time(value, axes, turns, split_dim, concat_dim):
    tiles = cut_along(value, split_dim, lax.axis_size(axes))
    return laid_out(turned_blocks(tiles, axes, turns), concat_dim)


def copy_for_each(value, axis):
    copies = jnp.broadcast_to(value, (lax.axis_size(axis), *value.shape))
    return lax.all_to_all(copies, axis, split_axis=0, concat_axis=0, tiled=True)


def taken_together(value, axis):
    return copy_for_each(value, axis).astype(jnp.float32).sum(axis=0)


def slope(diff, inv_sq):
    return -(diff * inv_sq) * jnp.exp(-0.5 * diff * diff * inv_sq)


def shards(
    coarse_latents,
    send_rows,
    up_index,
    up_weight,
    neighbors,
    live_counts,
    area,
    fine_skip,
    targets,
    kernel_width,
    w_in,
    w_out,
    ln_gain,
    w_head,
):
    dom_count = lax.axis_size("dom")
    mem_count = lax.axis_size(MEM)
    fine_rows = fine_skip.shape[0]
    width = fine_skip.shape[1]
    outgoing = coarse_latents[0][send_rows[0]]
    incoming = lax.all_to_all(outgoing, "dom", split_axis=0, concat_axis=0, tiled=True)
    table = incoming.reshape(dom_count * incoming.shape[1], width)
    unpooled = jnp.zeros((fine_rows, width), jnp.float32)
    for k in range(up_index.shape[0]):
        unpooled = unpooled + up_weight[k][:, None] * table[up_index[k]].astype(jnp.float32)
    latent = (fine_skip.astype(jnp.float32) + unpooled).astype(jnp.bfloat16)
    extended = extended_2(latent, (("dom", 0),), RIM)
    total = jnp.zeros((fine_rows, width), jnp.float32)
    for k in range(neighbors.shape[0]):
        total = total + extended[neighbors[k]].astype(jnp.float32)
    agg = (total / K_NB).astype(jnp.bfloat16)
    pre = jnp.dot(latent, w_in[:width], preferred_element_type=jnp.float32) + jnp.dot(
        agg, w_in[width:], preferred_element_type=jnp.float32
    )
    act = jax.nn.silu(pre).astype(jnp.bfloat16)
    upd = jnp.dot(act, w_out, preferred_element_type=jnp.float32)
    mean_upd = jnp.mean(upd, axis=1, keepdims=True)
    centred = upd - mean_upd
    var_upd = jnp.mean(centred * centred, axis=1, keepdims=True)
    hidden = (
        latent.astype(jnp.float32) + centred * lax.rsqrt(var_upd + 1e-05) * ln_gain[None, :]
    ).astype(jnp.bfloat16)
    pred = lax.dot_general(
        w_head, hidden, (((0,), (1,)), ((), ())), preferred_element_type=jnp.float32
    ).astype(jnp.bfloat16)
    inv_sq = (1.0 / (kernel_width * kernel_width))[:, None]
    local = jnp.arange(fine_rows, dtype=jnp.int32)
    weight = (area * (local < live_counts[0]).astype(jnp.float32))[None, :]
    share = fine_rows // mem_count
    first = lax.axis_index(MEM) * share
    members = one_axis_at_a_time(pred[None], MEM, (0, 1), 2, 0)
    members_f = members.astype(jnp.float32)
    target_share = lax.dynamic_slice_in_dim(targets, first, share, 1).astype(jnp.float32)
    weight_share = lax.dynamic_slice_in_dim(weight, first, share, 1)

    def add_member(j, inner):
        other = lax.dynamic_index_in_dim(members_f, j, 0, keepdims=True)
        return inner + slope(members_f - other, inv_sq)

    acc = lax.fori_loop(0, mem_count, add_member, jnp.zeros(members_f.shape, jnp.float32))
    scored = (
        weight_share[None] * (acc / mem_count - slope(members_f - target_share[None], inv_sq))
    ).astype(jnp.bfloat16)
    gscore = lax.all_to_all(scored, MEM, split_axis=0, concat_axis=2, tiled=True)[0]
    grad_latent = lax.dot_general(
        gscore, w_head, (((0,), (1,)), ((), ())), preferred_element_type=jnp.float32
    ).astype(jnp.bfloat16)
    head_term = lax.dot_general(
        hidden, gscore, (((0,), (1,)), ((), ())), preferred_element_type=jnp.float32
    )
    head_total = taken_together(head_term.astype(jnp.bfloat16), MEM).astype(jnp.float32)
    scale = 1.0 / math.sqrt(mem_count * fine_rows)
    return (grad_latent[None], (head_total * scale)[None])


def solution(mesh):
    finer = Mesh(mesh.devices.reshape(mesh.shape["dom"], 4, 4), ("dom", "mem_0", "mem_1"))
    in_specs = (
        P(MEM, "dom", None),
        P("dom", None, None),
        P(None, "dom"),
        P(None, "dom"),
        P(None, "dom"),
        P("dom"),
        P("dom"),
        P("dom", None),
        P(None, "dom"),
        P(),
        P(),
        P(),
        P(),
        P(),
    )
    out_specs = (P(MEM, "dom", None), P("dom", None, None))
    return jax.shard_map(
        shards, mesh=finer, in_specs=in_specs, out_specs=out_specs, check_vma=False
    )
```

profile of v0, /device:TPU:8, one launch (start us, length us, event | category | flops | bytes accessed | tf_op | source)
XLA Modules:
  0.0 271.2 jit_solution(13352311865496611565)
XLA Ops:
  0.6 0.8 fusion.18
  1.4 0.3 copy-done
  1.7 9.2 %gather_fusion = bf16[2048,512]{1,0:T(8,128)(2,1)} fusion(bf16[512,512]{1,0:T(8,128)(2,1)S(1)} %bitcast.76, s32[2048]{0:T(1024)S(1)} %fusion.18), kind=kCustom, calls=%fused_computation | custom fusion | bytes 4202496 | tf_op jit(solution)/shard_map/gather | solution.py:84
  10.9 8.6 %all-to-all-start = ((bf16[16,128,512]{2,1,0:T(8,128)(2,1)}), bf16[16,128,512]{2,1,0:T(8,128)(2,1)S(1)}, u32[]{:S(2)}, u32[]{:S(2)}) async-start(bf16[16,128,512]{2,1,0:T(8,128)(2,1)} %bitcast.80), calls=%async_computation | async-start | bytes 4194304 | tf_op jit(solution)/shard_map/all_to_all | solution.py:85
  19.5 4.0 %copy.68 = bf16[2048,512]{0,1:T(8,128)(2,1)} copy(bf16[2048,512]{1,0:T(8,128)(2,1)} %param.23) | data formatting | bytes 4194304 | tf_op args[7]
  23.8 44.9 %all-to-all-done = bf16[16,128,512]{2,1,0:T(8,128)(2,1)S(1)} async-done(((bf16[16,128,512]{2,1,0:T(8,128)(2,1)}), bf16[16,128,512]{2,1,0:T(8,128)(2,1)S(1)}, u32[]{:S(2)}, u32[]{:S(2)}) %all-to-all-start) | async-done | bytes 2097184 | tf_op jit(solution)/shard_map/all_to_all | solution.py:85
  68.7 9.2 %gather_fusion.1 = bf16[2048,512]{1,0:T(8,128)(2,1)} fusion(bf16[2048,512]{1,0:T(8,128)(2,1)S(1)} %bitcast.77, s32[2048]{0:T(1024)S(1)} %broadcast_clamp_fusion.8), kind=kCustom, calls=%fused_computation.1 | custom fusion | bytes 4202496 | tf_op jit(solution)/shard_map/gather | solution.py:89
  77.9 4.0 %copy.69 = bf16[2048,512]{0,1:T(8,128)(2,1)} copy(bf16[2048,512]{1,0:T(8,128)(2,1)} %gather_fusion.1) | data formatting | bytes 4194304 | tf_op jit(solution)/shard_map/gather | solution.py:89
  81.9 9.2 %gather_fusion.2 = bf16[2048,512]{1,0:T(8,128)(2,1)} fusion(bf16[2048,512]{1,0:T(8,128)(2,1)S(1)} %bitcast.78, s32[2048]{0:T(1024)S(1)} %broadcast_clamp_fusion.7), kind=kCustom, calls=%fused_computation.2 | custom fusion | bytes 4202496 | tf_op jit(solution)/shard_map/gather | solution.py:89
  91.1 4.0 %copy.70 = bf16[2048,512]{0,1:T(8,128)(2,1)} copy(bf16[2048,512]{1,0:T(8,128)(2,1)} %gather_fusion.2) | data formatting | bytes 4194304 | tf_op jit(solution)/shard_map/gather | solution.py:89
  95.0 9.2 %gather_fusion.3 = bf16[2048,512]{1,0:T(8,128)(2,1)} fusion(bf16[2048,512]{1,0:T(8,128)(2,1)S(1)} %bitcast.79, s32[2048]{0:T(1024)S(1)} %broadcast_clamp_fusion.6), kind=kCustom, calls=%fused_computation.3 | custom fusion | bytes 4202496 | tf_op jit(solution)/shard_map/gather | solution.py:89
  104.2 4.1 %copy.71 = bf16[2048,512]{0,1:T(8,128)(2,1)} copy(bf16[2048,512]{1,0:T(8,128)(2,1)} %gather_fusion.3) | data formatting | bytes 4194304 | tf_op jit(solution)/shard_map/gather | solution.py:89
  108.3 4.8 %add_convert_fusion.1 = bf16[2048,512]{0,1:T(8,128)(2,1)S(1)} fusion(bf16[2048,512]{0,1:T(8,128)(2,1)} %copy.71, bf16[2048,512]{0,1:T(8,128)(2,1)} %copy.70, bf16[2048,512]{0,1:T(8,128)(2,1)} %copy.69, bf16[2048,512]{0,1:T(8,128)(2,1)S(1)} %copy-done.5, f32[2048]{0:T(1024)S(1)} %bitcast.101, f32[2048]{0:T(1024)S(1)} %bitcast.102, f32[2048]{0:T(1024)S(1)} %bitcast.100), kind=kLoop, calls=%fused_computation.20 | loop fusion | flops 11534336 | bytes 10510336 | tf_op jit(solution)/shard_map/convert_element_type | solution.py:90
  113.2 2.1 collective-permute-start
  115.4 1.5 collective-permute-start.1
  116.9 3.3 %fusion.15 = f32[2048,512]{1,0:T(8,128)} fusion(bf16[2048,512]{0,1:T(8,128)(2,1)S(1)} %add_convert_fusion.1, bf16[1024,512]{1,0:T(8,128)(2,1)S(1)} %copy-done.7), kind=kOutput, calls=%fused_computation.38 | convolution fusion | flops 1073741824 | bytes 6815744 | tf_op jit(solution)/shard_map/dot_general | solution.py:96
  120.1 1.7 pad_maximum_fusion
  121.8 2.8 %copy.72 = bf16[2304,512]{1,0:T(8,128)(2,1)S(1)} copy(bf16[2304,512]{0,1:T(8,128)(2,1)} %pad_maximum_fusion) | data formatting | bytes 4718592 | tf_op jit(solution)/shard_map/concatenate | solution.py:23
  124.7 9.1 %gather_fusion.4 = bf16[2048,512]{1,0:T(8,128)(2,1)} fusion(bf16[2304,512]{1,0:T(8,128)(2,1)S(1)} %copy.72, s32[2048]{0:T(1024)S(1)} %broadcast_clamp_fusion.5), kind=kCustom, calls=%fused_computation.4 | custom fusion | bytes 4202496 | tf_op jit(solution)/shard_map/gather | solution.py:94
  133.8 9.1 %gather_fusion.5 = bf16[2048,512]{1,0:T(8,128)(2,1)} fusion(bf16[2304,512]{1,0:T(8,128)(2,1)S(1)} %copy.72, s32[2048]{0:T(1024)S(1)} %broadcast_clamp_fusion.4), kind=kCustom, calls=%fused_computation.5 | custom fusion | bytes 4202496 | tf_op jit(solution)/shard_map/gather | solution.py:94
  142.9 9.2 %gather_fusion.6 = bf16[2048,512]{1,0:T(8,128)(2,1)} fusion(bf16[2304,512]{1,0:T(8,128)(2,1)S(1)} %copy.72, s32[2048]{0:T(1024)S(1)} %broadcast_clamp_fusion.3), kind=kCustom, calls=%fused_computation.6 | custom fusion | bytes 4202496 | tf_op jit(solution)/shard_map/gather | solution.py:94
  152.1 9.2 %gather_fusion.7 = bf16[2048,512]{1,0:T(8,128)(2,1)} fusion(bf16[2304,512]{1,0:T(8,128)(2,1)S(1)} %copy.72, s32[2048]{0:T(1024)S(1)} %broadcast_clamp_fusion.2), kind=kCustom, calls=%fused_computation.7 | custom fusion | bytes 4202496 | tf_op jit(solution)/shard_map/gather | solution.py:94
  161.3 9.2 %gather_fusion.8 = bf16[2048,512]{1,0:T(8,128)(2,1)} fusion(bf16[2304,512]{1,0:T(8,128)(2,1)S(1)} %copy.72, s32[2048]{0:T(1024)S(1)} %broadcast_clamp_fusion.1), kind=kCustom, calls=%fused_computation.8 | custom fusion | bytes 4202496 | tf_op jit(solution)/shard_map/gather | solution.py:94
  170.4 9.2 %gather_fusion.9 = bf16[2048,512]{1,0:T(8,128)(2,1)} fusion(bf16[2304,512]{1,0:T(8,128)(2,1)S(1)} %copy.72, s32[2048]{0:T(1024)S(1)} %broadcast_clamp_fusion), kind=kCustom, calls=%fused_computation.9 | custom fusion | bytes 4202496 | tf_op jit(solution)/shard_map/gather | solution.py:94
  179.6 11.6 %fusion.24 = (f32[2048]{0:T(1024)S(1)}, f32[2048,512]{0,1:T(8,128)}) fusion(bf16[512,512]{1,0:T(8,128)(2,1)S(1)} %copy-done.12, f32[2048,512]{1,0:T(8,128)} %fusion.15, bf16[2048,512]{1,0:T(8,128)(2,1)} %gather_fusion.9, bf16[2048,512]{1,0:T(8,128)(2,1)} %gather_fusion.8, bf16[2048,512]{1,0:T(8,128)(2,1)} %gather_fusion.7, ...), kind=kOutput, calls=%fused_computation.73 | convolution fusion | flops 2168453120 | bytes 22028288 | tf_op jit(solution)/shard_map/dot_general | solution.py:100
  191.2 2.8 %multiply_reduce_fusion = f32[2048]{0:T(1024)S(1)} fusion(f32[2048,512]{0,1:T(8,128)} %get-tuple-element.128, f32[2048]{0:T(1024)S(1)} %broadcast_multiply_fusion.1), kind=kLoop, calls=%fused_computation.17 | loop fusion | flops 3143680 | bytes 4210688 | tf_op jit(solution)/shard_map/reduce_sum | solution.py:103
  194.0 3.3 %add_convert_fusion = bf16[2048,512]{0,1:T(8,128)(2,1)S(1)} fusion(bf16[2048,512]{0,1:T(8,128)(2,1)S(1)} %copy-done.2, f32[2048,512]{0,1:T(8,128)} %get-tuple-element.128, f32[512]{0:T(512)S(1)} %copy-done.11, f32[2048]{0:T(1024)S(1)} %add_rsqrt_fusion, f32[2048]{0:T(1024)S(1)} %broadcast_multiply_fusion.1), kind=kLoop, calls=%fused_computation.16 | loop fusion | flops 6291456 | bytes 8407040 | tf_op jit(solution)/shard_map/convert_element_type | solution.py:106
  197.3 1.3 copy-done.3
  198.7 0.5 convolution_convert_fusion.1
  199.2 0.9 copy.78
  200.1 4.9 %all-to-all-start.1 = ((bf16[4,4,1,83,128]{4,1,3,2,0:T(4,128)(2,1)}), bf16[4,4,1,83,128]{4,1,3,2,0:T(4,128)(2,1)S(1)}, u32[]{:S(2)}, u32[]{:S(2)}) async-start(bf16[4,4,1,83,128]{4,1,3,2,0:T(4,128)(2,1)} %copy.78), calls=%async_computation.1 | async-start | bytes 679936 | tf_op jit(solution)/shard_map/all_to_all | solution.py:42
  205.7 0.7 dynamic-slice_convert_fusion
  206.4 5.7 %all-to-all-done.1 = bf16[4,4,1,83,128]{4,1,3,2,0:T(4,128)(2,1)S(1)} async-done(((bf16[4,4,1,83,128]{4,1,3,2,0:T(4,128)(2,1)}), bf16[4,4,1,83,128]{4,1,3,2,0:T(4,128)(2,1)S(1)}, u32[]{:S(2)}, u32[]{:S(2)}) %all-to-all-start.1) | async-done | bytes 340000 | tf_op jit(solution)/shard_map/all_to_all | solution.py:42
  212.1 0.9 copy.79
  212.9 4.4 %all-to-all-start.2 = ((bf16[4,4,1,83,128]{4,0,3,2,1:T(4,128)(2,1)}), bf16[4,4,1,83,128]{4,0,3,2,1:T(4,128)(2,1)S(1)}, u32[]{:S(2)}, u32[]{:S(2)}) async-start(bf16[4,4,1,83,128]{4,0,3,2,1:T(4,128)(2,1)} %copy.79), calls=%async_computation.2 | async-start | bytes 679936 | tf_op jit(solution)/shard_map/all_to_all | solution.py:42
  217.3 0.8 compare_select_fusion.10
  218.1 7.0 %all-to-all-done.2 = bf16[4,4,1,83,128]{4,0,3,2,1:T(4,128)(2,1)S(1)} async-done(((bf16[4,4,1,83,128]{4,0,3,2,1:T(4,128)(2,1)}), bf16[4,4,1,83,128]{4,0,3,2,1:T(4,128)(2,1)S(1)}, u32[]{:S(2)}, u32[]{:S(2)}) %all-to-all-start.2) | async-done | bytes 340000 | tf_op jit(solution)/shard_map/all_to_all | solution.py:42
  225.3 0.2 copy.81
  225.5 7.5 %while.14 = (s32[]{:T(128)}, f32[16,83,128]{2,1,0:T(8,128)S(1)}, f32[16,83,128]{2,1,0:T(8,128)S(1)}, f32[83]{0:T(128)S(1)}, s32[]{:T(128)}, /*index=5*/s32[]{:T(128)}) while((s32[]{:T(128)}, f32[16,83,128]{2,1,0:T(8,128)S(1)}, f32[16,83,128]{2,1,0:T(8,128)S(1)}, f32[83]{0:T(128)S(1)}, s32[]{:T(128)}, /*index=5*/s32[]{:T(128)}) %tuple.49), condition=%wide.region_3.4_spmd.clone, body=%wide.region_2.3_spmd.clone.sunk | while | flops 1529859 | bytes 2167711 | solution.py:124
  225.5 0.4 fusion.36
  226.0 0.4 fusion.36
  226.5 0.4 fusion.36
  226.9 0.4 fusion.36
  227.4 0.4 fusion.36
  227.9 0.4 fusion.36
  228.3 0.4 fusion.36
  228.8 0.4 fusion.36
  229.3 0.4 fusion.36
  229.8 0.4 fusion.36
  230.2 0.4 fusion.36
  230.7 0.4 fusion.36
  231.2 0.4 fusion.36
  231.6 0.4 fusion.36
  232.1 0.4 fusion.36
  232.6 0.4 fusion.36
  233.0 0.4 fusion.12
  233.5 11.6 %all_to_all.35 = bf16[16,83,128]{2,1,0:T(8,128)(2,1)S(1)} all-to-all(bf16[16,83,128]{2,1,0:T(8,128)(2,1)S(1)} %copy.83), channel_id=1, replica_groups=mesh['dom'=16,'mem_0'=4,'mem_1'=4] {'mem_0','mem_1'}, dimensions={0} | all-to-all | bytes 679936 | tf_op jit(solution)/shard_map/all_to_all | solution.py:128
  245.3 0.8 convolution_convert_fusion.2
  246.1 1.2 broadcast_in_dim.8
  247.3 5.7 %all-to-all-start.4 = ((bf16[16,512,83]{1,2,0:T(8,128)(2,1)}), bf16[16,512,83]{1,2,0:T(8,128)(2,1)S(1)}, u32[]{:S(2)}, u32[]{:S(2)}) async-start(bf16[16,512,83]{1,2,0:T(8,128)(2,1)} %broadcast_in_dim.8), calls=%async_computation.4 | async-start | bytes 2883584 | tf_op jit(solution)/shard_map/all_to_all | solution.py:53
  253.0 2.1 fusion.4
  255.0 15.2 %all-to-all-done.4 = bf16[16,512,83]{1,2,0:T(8,128)(2,1)S(1)} async-done(((bf16[16,512,83]{1,2,0:T(8,128)(2,1)}), bf16[16,512,83]{1,2,0:T(8,128)(2,1)S(1)}, u32[]{:S(2)}, u32[]{:S(2)}) %all-to-all-start.4) | async-done | bytes 1359904 | tf_op jit(solution)/shard_map/all_to_all | solution.py:53
  270.2 0.2 convert_reduce_fusion
  270.4 0.8 mul.192
  (69 shorter events, 1.0 us)
Async XLA Ops:
  0.6 1.1 copy-start
  10.9 57.8 %all-to-all-start = ((bf16[16,128,512]{2,1,0:T(8,128)(2,1)}), bf16[16,128,512]{2,1,0:T(8,128)(2,1)S(1)}, u32[]{:S(2)}, u32[]{:S(2)}) async-start(bf16[16,128,512]{2,1,0:T(8,128)(2,1)} %bitcast.80), calls=%async_computation | async-start | bytes 4194304 | tf_op jit(solution)/shard_map/all_to_all | solution.py:85
  19.5 4.0 %copy-start.9 = (s32[3,2048]{1,0:T(4,128)S(1)}, s32[3,2048]{1,0:T(4,128)}, u32[]{:S(2)}) copy-start(s32[3,2048]{1,0:T(4,128)} %param.18) | copy-start | bytes 73732
  19.5 4.1 %copy-start.8 = (s32[6,2048]{1,0:T(8,128)S(1)}, s32[6,2048]{1,0:T(8,128)}, u32[]{:S(2)}) copy-start(s32[6,2048]{1,0:T(8,128)} %param.20) | copy-start | bytes 147460
  19.5 4.2 %copy-start.10 = (f32[3,2048]{1,0:T(4,128)S(1)}, f32[3,2048]{1,0:T(4,128)}, u32[]{:S(2)}) copy-start(f32[3,2048]{1,0:T(4,128)} %param.19) | copy-start | bytes 73732
  104.2 4.1 %copy-start.5 = (bf16[2048,512]{0,1:T(8,128)(2,1)S(1)}, bf16[2048,512]{0,1:T(8,128)(2,1)}, u32[]{:S(2)}) copy-start(bf16[2048,512]{0,1:T(8,128)(2,1)} %copy.68) | copy-start | bytes 6291460
  108.3 8.5 %copy-start.7 = (bf16[1024,512]{1,0:T(8,128)(2,1)S(1)}, bf16[1024,512]{1,0:T(8,128)(2,1)}, u32[]{:S(2)}) copy-start(bf16[1024,512]{1,0:T(8,128)(2,1)} %param.26) | copy-start | bytes 3145732
  113.2 7.0 %copy-start.1 = (bf16[2048,512]{0,1:T(8,128)(2,1)}, bf16[2048,512]{0,1:T(8,128)(2,1)S(1)}, u32[]{:S(2)}) copy-start(bf16[2048,512]{0,1:T(8,128)(2,1)S(1)} %add_convert_fusion.1) | copy-start | bytes 6291460
  113.2 6.9 %collective-permute-start = (bf16[128,512]{0,1:T(8,128)(2,1)S(1)}, bf16[128,512]{0,1:T(8,128)(2,1)S(1)}, u32[]{:S(2)}, u32[]{:S(2)}) collective-permute-start(bf16[128,512]{0,1:T(8,128)(2,1)S(1)} %get-tuple-element.113), channel_id=1, source_target_pairs={{0,16},{16,32},{32,48},{48,64},{64,80},{80,96},{96,112},{112,128},... | collective-permute-start | bytes 393224 | tf_op jit(solution)/shard_map/ppermute | solution.py:21
  115.4 4.7 %collective-permute-start.1 = (bf16[128,512]{0,1:T(8,128)(2,1)S(1)}, bf16[128,512]{0,1:T(8,128)(2,1)S(1)}, u32[]{:S(2)}, u32[]{:S(2)}) collective-permute-start(bf16[128,512]{0,1:T(8,128)(2,1)S(1)} %get-tuple-element.114), channel_id=1, source_target_pairs={{16,0},{32,16},{48,32},{64,48},{80,64},{96,80},{112,96},{128,112},... | collective-permute-start | bytes 393224 | tf_op jit(solution)/shard_map/ppermute | solution.py:22
  170.4 9.2 %copy-start.12 = (bf16[512,512]{1,0:T(8,128)(2,1)S(1)}, bf16[512,512]{1,0:T(8,128)(2,1)}, u32[]{:S(2)}) copy-start(bf16[512,512]{1,0:T(8,128)(2,1)} %param.27) | copy-start | bytes 1572868
  191.1 2.9 %copy-start.2 = (bf16[2048,512]{0,1:T(8,128)(2,1)S(1)}, bf16[2048,512]{0,1:T(8,128)(2,1)}, u32[]{:S(2)}) copy-start(bf16[2048,512]{0,1:T(8,128)(2,1)} %copy-done.1) | copy-start | bytes 6291460
  191.1 2.9 %copy-start.11 = (f32[512]{0:T(512)S(1)}, f32[512]{0:T(512)}, u32[]{:S(2)}) copy-start(f32[512]{0:T(512)} %param.28) | copy-start | bytes 6148
  194.0 4.7 %copy-start.6 = (bf16[512,83]{0,1:T(8,128)(2,1)S(1)}, bf16[512,83]{0,1:T(8,128)(2,1)}, u32[]{:S(2)}) copy-start(bf16[512,83]{0,1:T(8,128)(2,1)} %param.29) | copy-start | bytes 254980
  197.3 1.3 copy-start.3
  199.1 19.0 %copy-start.13 = (f32[83]{0:T(128)S(1)}, f32[83]{0:T(128)}, u32[]{:S(2)}) copy-start(f32[83]{0:T(128)} %param.25) | copy-start | bytes 1000
  200.1 12.0 %all-to-all-start.1 = ((bf16[4,4,1,83,128]{4,1,3,2,0:T(4,128)(2,1)}), bf16[4,4,1,83,128]{4,1,3,2,0:T(4,128)(2,1)S(1)}, u32[]{:S(2)}, u32[]{:S(2)}) async-start(bf16[4,4,1,83,128]{4,1,3,2,0:T(4,128)(2,1)} %copy.78), calls=%async_computation.1 | async-start | bytes 679936 | tf_op jit(solution)/shard_map/all_to_all | solution.py:42
  212.9 12.2 %all-to-all-start.2 = ((bf16[4,4,1,83,128]{4,0,3,2,1:T(4,128)(2,1)}), bf16[4,4,1,83,128]{4,0,3,2,1:T(4,128)(2,1)S(1)}, u32[]{:S(2)}, u32[]{:S(2)}) async-start(bf16[4,4,1,83,128]{4,0,3,2,1:T(4,128)(2,1)} %copy.79), calls=%async_computation.2 | async-start | bytes 679936 | tf_op jit(solution)/shard_map/all_to_all | solution.py:42
  233.4 11.9 %copy-start.4 = (bf16[2048,512]{0,1:T(8,128)(2,1)S(1)}, bf16[2048,512]{0,1:T(8,128)(2,1)}, u32[]{:S(2)}) copy-start(bf16[2048,512]{0,1:T(8,128)(2,1)} %copy-done.3) | copy-start | bytes 6291460
  247.3 22.9 %all-to-all-start.4 = ((bf16[16,512,83]{1,2,0:T(8,128)(2,1)}), bf16[16,512,83]{1,2,0:T(8,128)(2,1)S(1)}, u32[]{:S(2)}, u32[]{:S(2)}) async-start(bf16[16,512,83]{1,2,0:T(8,128)(2,1)} %broadcast_in_dim.8), calls=%async_computation.4 | async-start | bytes 2883584 | tf_op jit(solution)/shard_map/all_to_all | solution.py:53
where the time goes:
time: 276 us; the launch traced here: 271 us
  local copies, waits for them, and re-layouts  117 us (42%)
  waiting for transfers between devices  72.8 us (26%)
  starting transfers between devices  27.2 us (10%)
  other arithmetic  22.5 us (8%)
  matrix products  18.1 us (7%)
  blocking collectives  11.6 us (4%)
    gather x6, local copies, waits for them, and re-layouts, shards(): total = total + extended[neighbors[k]].astype(jnp.float32)  54.9 us
    all_to_all x1, waiting for transfers between devices, shards(): lax.all_to_all(outgoing, 'dom', split_axis=0, concat_axis=0, tiled=True)  44.9 us
    gather x6, local copies, waits for them, and re-layouts, shards(): table[up_index[k]].astype(jnp.float32)  39.6 us
    all_to_all x1, waiting for transfers between devices, copy_for_each(): return lax.all_to_all(copies, axis, split_axis=0, concat_axis=0, tiled=True)  15.2 us
    all_to_all x2, waiting for transfers between devices, turned_blocks(): lax.all_to_all(tiles, axes[k], split_axis=k, concat_axis=k, tiled=True)  12.7 us
    all_to_all x1, blocking collectives, shards(): lax.all_to_all(scored, MEM, split_axis=0, concat_axis=2, tiled=True)[0]  11.6 us
    dot_general x1, matrix products, shards(): upd = jnp.dot(act, w_out, preferred_element_type=jnp.float32)  11.6 us
    all_to_all x2, starting transfers between devices, turned_blocks(): lax.all_to_all(tiles, axes[k], split_axis=k, concat_axis=k, tiled=True)  9.32 us
  transfers between devices with their start and end apart: 6, of which 4 were waited for; matrix products, arithmetic and copies ran while one was open for 4% of the time, Pallas kernels for 0%

commit v1 on v0

v1 whole, which is shorter than its diff:
```python
import functools
import math

import jax
import jax.numpy as jnp
from jax import lax
from jax.experimental import pallas as pl
from jax.experimental.pallas import tpu as pltpu
from jax.sharding import PartitionSpec as P

F32 = jnp.float32
BF16 = jnp.bfloat16
VARS = 83
VP = 96
NT = (((1,), (1,)), ((), ()))


def lanes_of(row):
    return jnp.broadcast_to(row, (128, 128)).T


def kernel(
    coarse,
    send_rows,
    up_index,
    up_weight,
    neighbors,
    live,
    area,
    skip,
    targets,
    kwidth,
    w_in,
    w_out,
    gain,
    w_head,
    gs_out,
    head_out,
    tiles,
    rows,
    wbuf,
    nbuf,
    cols,
    recv,
    sbuf,
    sibbuf,
    acc,
    skipv,
    ext,
    hidden,
    win,
    wout,
    whp,
    wht,
    kwp,
    inv_b,
    tgt,
    psend,
    pall,
    pf,
    ssend,
    gs,
    hp,
    hr,
    hs,
    hall,
    loc_sem,
    tile_s,
    tile_r,
    rows_s,
    rows_r,
    g_s,
    sib_s,
    recv_sem,
    rim_s,
    rim_r,
    pred_s,
    pred_r,
    gs_s,
    gs_r,
    hr_s,
    hr_r,
    ha_s,
    ha_r,
):
    me_d = lax.axis_index("dom")
    me_m = lax.axis_index("mem")
    c = me_d // 2
    k = me_d - 2 * c
    other = 1 - k

    def chip(offset):
        return lax.rem(c + offset + 8, 8)

    def member(offset):
        return lax.rem(me_m + offset + 16, 16)

    def remote(src, dst, ssem, rsem, **device):
        return pltpu.make_async_remote_copy(
            src_ref=src,
            dst_ref=dst,
            send_sem=ssem,
            recv_sem=rsem,
            device_id=device,
            device_id_type=pl.DeviceIdType.MESH,
        )

    barrier = pltpu.get_barrier_semaphore()

    def greet(r, carry):
        pl.semaphore_signal(
            barrier,
            inc=1,
            device_id={"dom": lax.rem(me_d + r, 16)},
            device_id_type=pl.DeviceIdType.MESH,
        )
        pl.semaphore_signal(
            barrier, inc=1, device_id={"mem": member(r)}, device_id_type=pl.DeviceIdType.MESH
        )
        return carry

    lax.fori_loop(1, 16, greet, 0)
    loads = [
        pltpu.make_async_copy(coarse, tiles.at[0], loc_sem.at[0]),
        pltpu.make_async_copy(skip, skipv, loc_sem.at[1]),
        pltpu.make_async_copy(w_in, win, loc_sem.at[2]),
        pltpu.make_async_copy(w_out, wout, loc_sem.at[3]),
    ]
    for load in loads:
        load.start()
    pl.semaphore_wait(barrier, 30)

    to_right = [
        remote(coarse, tiles.at[1], tile_s.at[0], tile_r.at[0], dom=chip(1) * 2 + k),
        remote(send_rows, rows.at[0], rows_s.at[0], rows_r.at[0], dom=chip(1) * 2 + k),
    ]
    to_left = [
        remote(coarse, tiles.at[2], tile_s.at[1], tile_r.at[1], dom=chip(-1) * 2 + k),
        remote(send_rows, rows.at[1], rows_s.at[1], rows_r.at[1], dom=chip(-1) * 2 + k),
    ]
    for copy in to_right + to_left:
        copy.start()

    lane = lax.broadcasted_iota(jnp.int32, (128, 128), 1).astype(F32)

    def picked(table, tile, dest):
        row = table[pl.ds(dest, 1), :].astype(F32)
        col = lanes_of(row)
        hot = jnp.concatenate(
            [jnp.where(col == lane + 128.0 * q, 1.0, 0.0).astype(BF16) for q in range(4)], axis=1
        )
        return jnp.dot(hot, tile[...], preferred_element_type=F32).astype(BF16)

    my_rows = pl.ds(pl.multiple_of(k * 128, 128), 128)

    def at_home(table, tile, slot, rel):
        sibbuf[slot] = picked(table, tile, me_d + other - k)
        copy = remote(
            sibbuf.at[slot],
            recv.at[rel, my_rows],
            sib_s.at[slot],
            recv_sem.at[rel, k],
            dom=c * 2 + other,
        )
        copy.start()
        recv[rel, my_rows, :] = picked(table, tile, me_d)
        return copy

    loads[0].wait()
    sib_copies = [at_home(send_rows, tiles.at[0], 0, 0)]

    def weights_of(t, carry):
        at = pl.ds(pl.multiple_of(t * 128, 128), 128)
        for j in range(3):
            cols[j] = lanes_of(up_index[j : j + 1, at].astype(F32))
            cols[3 + j] = lanes_of(up_weight[j : j + 1, at])

        def part(s, carry):
            sub = pl.ds(pl.multiple_of(s * 32, 32), 32)
            out = pl.ds(pl.multiple_of(t * 128 + s * 32, 32), 32)
            idx = [cols[j, sub, :] for j in range(3)]
            wgt = [cols[3 + j, sub, :] for j in range(3)]
            base = lax.broadcasted_iota(jnp.int32, (32, 128), 1).astype(F32)
            for q in range(16):
                slot = base + 128.0 * q
                w = (
                    jnp.where(idx[0] == slot, wgt[0], 0.0)
                    + jnp.where(idx[1] == slot, wgt[1], 0.0)
                    + jnp.where(idx[2] == slot, wgt[2], 0.0)
                )
                hi = w.astype(BF16)
                lo = (w - hi.astype(F32)).astype(BF16)
                wbuf[q // 2, out, (q % 2) * 128 : (q % 2) * 128 + 128] = hi
                wbuf[q // 2, out, 256 + (q % 2) * 128 : 384 + (q % 2) * 128] = lo
            return carry

        lax.fori_loop(0, 4, part, 0)
        return carry

    lax.fori_loop(0, 16, weights_of, 0)

    def counts_of(t, carry):
        at = pl.ds(pl.multiple_of(t * 128, 128), 128)
        shift = ((t // 2) * 256).astype(F32)
        for j in range(6):
            cols[j] = lanes_of(neighbors[j : j + 1, at].astype(F32) - shift)

        def part(s, carry):
            sub = pl.ds(pl.multiple_of(s * 32, 32), 32)
            out = pl.ds(pl.multiple_of(t * 128 + s * 32, 32), 32)
            idx = [cols[j, sub, :] for j in range(6)]
            base = lax.broadcasted_iota(jnp.int32, (32, 128), 1).astype(F32)
            for q in range(4):
                spot = base + 128.0 * q
                total = jnp.where(idx[0] == spot, 1.0, 0.0)
                for j in range(1, 6):
                    total = total + jnp.where(idx[j] == spot, 1.0, 0.0)
                nbuf[out, q * 128 : q * 128 + 128] = total.astype(BF16)
            return carry

        lax.fori_loop(0, 4, part, 0)
        return carry

    whp[...] = jnp.zeros((512, 128), F32)
    whp[:, :VARS] = w_head[...].astype(F32)
    for q in range(4):
        wht[:, q * 128 : q * 128 + 128] = whp[q * 128 : q * 128 + 128, :].T[:VP].astype(BF16)
    kwp[...] = jnp.ones((8, 128), F32)
    kwp[0:1, :VARS] = kwidth[...]
    width = kwp[0:1, :]
    inv_b[...] = lanes_of(1.0 / (width * width))[:VP]
    my_share = pl.ds(pl.multiple_of(me_m * 128, 128), 128)
    tgt[...] = jnp.zeros((VP, 128), F32)
    tgt[:VARS, :] = targets[:, my_share].astype(F32)

    lax.fori_loop(0, 16, counts_of, 0)

    for copy in to_right + to_left:
        copy.wait_recv()

    def far_copy(side, j, o, kd):
        dest = chip(o) * 2 + kd
        rel = 4 + (j + 1) // 2 if side == 0 else 4 - (j + 1) // 2
        return dest, remote(
            sbuf.at[side, j],
            recv.at[rel, my_rows],
            g_s.at[side, j],
            recv_sem.at[rel, k],
            dom=dest,
        )

    def both_ways(j, carry):
        o = 3 - (j + 1) // 2
        even = lax.rem(j, 2)
        for side in range(2):
            dest, copy = far_copy(side, j, o if side == 0 else -o, even if side == 0 else 1 - even)
            sbuf[side, j] = picked(rows.at[side], tiles.at[1 + side], dest)
            copy.start()
        return carry

    lax.fori_loop(0, 5, both_ways, 0)
    sib_copies.append(at_home(rows.at[0], tiles.at[1], 1, 7))
    sib_copies.append(at_home(rows.at[1], tiles.at[2], 2, 1))

    loads[1].wait()

    def arrived(rel, kb):
        half = pl.ds(pl.multiple_of(kb * 128, 128), 128)
        remote(
            sibbuf.at[0], recv.at[rel, half], sib_s.at[0], recv_sem.at[rel, kb], dom=c * 2 + other
        ).wait_recv()

    def added(rel, t, first):
        at = pl.ds(pl.multiple_of(t * 256, 256), 256)
        table = recv[rel]
        here = chip(rel)
        total = jnp.dot(wbuf[here, at, :256], table, preferred_element_type=F32)
        total = total + jnp.dot(wbuf[here, at, 256:], table, preferred_element_type=F32)
        before = skipv[at, :].astype(F32) if first else acc[at, :]
        return at, before + total

    for rel in (0, 7, 1, 6, 2, 5, 3):
        arrived(rel, other)
        if rel not in (0, 7, 1):
            arrived(rel, k)

        def accumulate(t, carry, rel=rel):
            at, total = added(rel, t, rel == 0)
            acc[at, :] = total
            return carry

        lax.fori_loop(0, 8, accumulate, 0)

    arrived(4, 0)
    arrived(4, 1)

    def finish(t, carry):
        at, total = added(4, t, False)
        ext[pl.ds(pl.multiple_of(t * 256 + 128, 128), 256), :] = total.astype(BF16)
        return carry

    lax.fori_loop(0, 2, lambda t, carry: finish(t * 7, carry), 0)
    rims = [
        remote(
            ext.at[pl.ds(2048, 128)],
            ext.at[pl.ds(0, 128)],
            rim_s.at[0],
            rim_r.at[0],
            dom=lax.rem(me_d + 1, 16),
        ),
        remote(
            ext.at[pl.ds(128, 128)],
            ext.at[pl.ds(2176, 128)],
            rim_s.at[1],
            rim_r.at[1],
            dom=lax.rem(me_d + 15, 16),
        ),
    ]
    for rim in rims:
        rim.start()
    lax.fori_loop(1, 7, finish, 0)
    loads[2].wait()
    loads[3].wait()

    gain_row = gain[...]

    def pred_copy(j):
        r = lax.rem(j - me_m + 16, 16)
        return r, remote(psend.at[j], pall.at[r], pred_s.at[r], pred_r.at[r], mem=j)

    def dense(i, carry):
        at = pl.ds(pl.multiple_of(i * 256 + 128, 128), 256)
        x = ext[at, :]
        total = jnp.dot(
            nbuf[pl.ds(pl.multiple_of(i * 256, 256), 256), :],
            ext[pl.ds(pl.multiple_of(i * 256, 256), 512), :],
            preferred_element_type=F32,
        )
        agg = (total / 6.0).astype(BF16)
        pre = jnp.dot(x, win[:512], preferred_element_type=F32) + jnp.dot(
            agg, win[512:], preferred_element_type=F32
        )
        half = 0.5 * pre
        act = (half + half * jnp.tanh(half)).astype(BF16)
        upd = jnp.dot(act, wout[...], preferred_element_type=F32)
        mean = jnp.sum(upd, axis=1, keepdims=True) * (1.0 / 512)
        centred = upd - mean
        var = jnp.sum(centred * centred, axis=1, keepdims=True) * (1.0 / 512)
        h = (x.astype(F32) + centred * lax.rsqrt(var + 1e-05) * gain_row).astype(BF16)
        hidden[pl.ds(pl.multiple_of(i * 256, 256), 256), :] = h
        pred = lax.dot_general(wht[...], h, NT, preferred_element_type=F32).astype(BF16)
        for s in range(2):
            j = 2 * i + s
            r, copy = pred_copy(j)
            psend[j] = pred[:, s * 128 : s * 128 + 128]

            @pl.when(r != 0)
            def _():
                copy.start()

            @pl.when(r == 0)
            def _():
                pall[0] = psend[j]

        return carry

    lax.fori_loop(1, 7, dense, 0)
    for rim in rims:
        rim.wait()

    @pl.when(me_d == 0)
    def _():
        ext[pl.ds(0, 128), :] = jnp.zeros((128, 512), BF16)

    @pl.when(me_d == 15)
    def _():
        ext[pl.ds(2176, 128), :] = jnp.zeros((128, 512), BF16)

    lax.fori_loop(0, 2, lambda t, carry: dense(t * 7, carry), 0)

    def pred_wait(r, carry):
        remote(psend.at[0], pall.at[r], pred_s.at[r], pred_r.at[r], mem=member(r)).wait_recv()
        return carry

    lax.fori_loop(1, 16, pred_wait, 0)

    def widen(r, carry):
        pf[r] = pall[r].astype(F32)
        return carry

    lax.fori_loop(0, 16, widen, 0)
    place = lax.broadcasted_iota(jnp.int32, (1, 128), 1) + me_m * 128
    weight = jnp.broadcast_to(jnp.where(place < live[0], area[:, my_share], 0.0), (8, 128))

    def scores(q, carry):
        at = pl.ds(pl.multiple_of(q * 8, 8), 8)
        inv = inv_b[at, :]
        halved = -0.5 * inv
        p = [pf[i, at, :] for i in range(16)]
        t = tgt[at, :]
        total = [None] * 16
        for i in range(16):
            for j in range(i):
                e = p[i] - p[j]
                s = e * jnp.exp(e * e * halved)
                total[i] = s if total[i] is None else total[i] + s
                total[j] = -s if total[j] is None else total[j] - s
        scale = weight * inv
        for i in range(16):
            e = p[i] - t
            pf[i, at, :] = scale * (e * jnp.exp(e * e * halved) - total[i] * (1.0 / 16))
        return carry

    lax.fori_loop(0, VP // 8, scores, 0)
    gs[:, my_share] = pf[0].astype(BF16)

    def gs_copy(r):
        return remote(ssend.at[r], gs.at[:, my_share], gs_s.at[r], gs_r.at[r], mem=member(-r))

    def give_back(r, carry):
        ssend[r] = pf[r].astype(BF16)
        gs_copy(r).start()
        return carry

    lax.fori_loop(1, 16, give_back, 0)

    def gs_wait(r, carry):
        share = pl.ds(pl.multiple_of(member(r) * 128, 128), 128)
        remote(ssend.at[r], gs.at[:, share], gs_s.at[r], gs_r.at[r], mem=member(r)).wait_recv()
        return carry

    lax.fori_loop(1, 16, gs_wait, 0)

    head = jnp.dot(gs[...], hidden[...], preferred_element_type=F32)
    for j in range(16):
        hp[j] = head[24 * (j // 4) : 24 * (j // 4) + 24, 128 * (j % 4) : 128 * (j % 4) + 128]

    def hr_copy(r):
        return remote(hp.at[member(r)], hr.at[r], hr_s.at[r], hr_r.at[r], mem=member(r))

    def spread(r, carry):
        hr_copy(r).start()
        return carry

    lax.fori_loop(1, 16, spread, 0)
    hr[0] = hp[me_m]
    gs_out[...] = gs[:VARS, :]

    def hr_wait(r, carry):
        hr_copy(r).wait_recv()
        return carry

    lax.fori_loop(1, 16, hr_wait, 0)
    summed = hr[0]
    for r in range(1, 16):
        summed = summed + hr[r]
    summed = summed * (1.0 / math.sqrt(32768))
    hs[...] = summed
    hall[me_m] = summed

    def ha_copy(r, owner):
        return remote(hs, hall.at[owner], ha_s.at[r], ha_r.at[r], mem=member(r))

    def tell(r, carry):
        ha_copy(r, me_m).start()
        return carry

    lax.fori_loop(1, 16, tell, 0)

    def ha_wait(r, carry):
        ha_copy(r, member(-r)).wait_recv()
        return carry

    lax.fori_loop(1, 16, ha_wait, 0)
    for j in range(16):
        lo = 24 * (j // 4)
        n = min(24, VARS - lo)
        head_out[lo : lo + n, 128 * (j % 4) : 128 * (j % 4) + 128] = hall[j, :n]

    for copy in to_right + to_left + sib_copies:
        copy.wait_send()

    def far_done(j, carry):
        o = 3 - (j + 1) // 2
        even = lax.rem(j, 2)
        for side in range(2):
            far_copy(side, j, o if side == 0 else -o, even if side == 0 else 1 - even)[
                1
            ].wait_send()
        return carry

    lax.fori_loop(0, 5, far_done, 0)

    def members_done(r, carry):
        pred_copy(member(r))[1].wait_send()
        gs_copy(r).wait_send()
        hr_copy(r).wait_send()
        ha_copy(r, me_m).wait_send()
        return carry

    lax.fori_loop(1, 16, members_done, 0)


def shards(
    coarse_latents,
    send_rows,
    up_index,
    up_weight,
    neighbors,
    live_counts,
    area,
    fine_skip,
    targets,
    kernel_width,
    w_in,
    w_out,
    ln_gain,
    w_head,
):
    hbm = pl.BlockSpec(memory_space=pl.ANY)
    vmem = pl.BlockSpec(memory_space=pltpu.VMEM)
    smem = pl.BlockSpec(memory_space=pltpu.SMEM)
    dma = pltpu.SemaphoreType.DMA
    gscore, head = pl.pallas_call(
        kernel,
        name="decoder_tail",
        out_shape=(
            jax.ShapeDtypeStruct((VARS, 2048), BF16),
            jax.ShapeDtypeStruct((VARS, 512), F32),
        ),
        in_specs=[hbm, vmem, vmem, vmem, vmem, smem, vmem, hbm, vmem, vmem, hbm, hbm, vmem, vmem],
        out_specs=(vmem, vmem),
        scratch_shapes=[
            pltpu.VMEM((3, 512, 512), BF16),
            pltpu.VMEM((2, 16, 128), jnp.int32),
            pltpu.VMEM((8, 2048, 512), BF16),
            pltpu.VMEM((2048, 512), BF16),
            pltpu.VMEM((6, 128, 128), F32),
            pltpu.VMEM((8, 256, 512), BF16),
            pltpu.VMEM((2, 5, 128, 512), BF16),
            pltpu.VMEM((3, 128, 512), BF16),
            pltpu.VMEM((2048, 512), F32),
            pltpu.VMEM((2048, 512), BF16),
            pltpu.VMEM((2304, 512), BF16),
            pltpu.VMEM((2048, 512), BF16),
            pltpu.VMEM((1024, 512), BF16),
            pltpu.VMEM((512, 512), BF16),
            pltpu.VMEM((512, 128), F32),
            pltpu.VMEM((VP, 512), BF16),
            pltpu.VMEM((8, 128), F32),
            pltpu.VMEM((VP, 128), F32),
            pltpu.VMEM((VP, 128), F32),
            pltpu.VMEM((16, VP, 128), BF16),
            pltpu.VMEM((16, VP, 128), BF16),
            pltpu.VMEM((16, VP, 128), F32),
            pltpu.VMEM((16, VP, 128), BF16),
            pltpu.VMEM((VP, 2048), BF16),
            pltpu.VMEM((16, 24, 128), F32),
            pltpu.VMEM((16, 24, 128), F32),
            pltpu.VMEM((24, 128), F32),
            pltpu.VMEM((16, 24, 128), F32),
            dma((4,)),
            dma((2,)),
            dma((2,)),
            dma((2,)),
            dma((2,)),
            dma((2, 5)),
            dma((3,)),
            dma((8, 2)),
            dma((2,)),
            dma((2,)),
            dma((16,)),
            dma((16,)),
            dma((16,)),
            dma((16,)),
            dma((16,)),
            dma((16,)),
            dma((16,)),
            dma((16,)),
        ],
        compiler_params=pltpu.CompilerParams(
            collective_id=0, has_side_effects=True, vmem_limit_bytes=60 * 1024 * 1024
        ),
    )(
        coarse_latents[0],
        send_rows[0],
        up_index,
        up_weight,
        neighbors,
        live_counts,
        area[None],
        fine_skip,
        targets,
        kernel_width[None],
        w_in,
        w_out,
        ln_gain[None],
        w_head,
    )
    grad_latent = lax.dot_general(
        gscore, w_head, (((0,), (1,)), ((), ())), preferred_element_type=F32
    ).astype(BF16)
    return grad_latent[None], head.T[None]


def solution(mesh):
    in_specs = (
        P("mem", "dom", None),
        P("dom", None, None),
        P(None, "dom"),
        P(None, "dom"),
        P(None, "dom"),
        P("dom"),
        P("dom"),
        P("dom", None),
        P(None, "dom"),
        P(),
        P(),
        P(),
        P(),
        P(),
    )
    out_specs = (P("mem", "dom", None), P("dom", None, None))
    return jax.shard_map(
        shards, mesh=mesh, in_specs=in_specs, out_specs=out_specs, check_vma=False
    )
```

time: 276 us -> 115 us (0.42); the launches traced: 271 us -> 115 us
  local copies, waits for them, and re-layouts: 117 us -> 3.43 us
  Pallas kernels: 0 us -> 107 us
  waiting for transfers between devices: 72.8 us -> 0 us
  starting transfers between devices: 27.2 us -> 0 us
  other arithmetic: 22.5 us -> 0 us
  matrix products: 18.1 us -> 3.04 us
  blocking collectives: 11.6 us -> 0 us
    pallas_call x0 -> x1, Pallas kernels: none -> 107 us  [shards(): pl.pallas_call(kernel, name='decoder_tail', out_shape=(jax.ShapeDtypeStru...]
    gather x13 -> x0, local copies, waits for them, and re-layouts: 104 us -> none  [the longest x6 54.9 us: shards(): total = total + extended[neighbors[k]].astype(jnp.float32)]
    all_to_all x4 -> x0, waiting for transfers between devices: 72.8 us -> none  [the longest x1 44.9 us: shards(): lax.all_to_all(outgoing, 'dom', split_axis=0, concat_axis=0, tiled=True)]
    all_to_all x4 -> x0, starting transfers between devices: 23.6 us -> none  [the longest x2 9.32 us: turned_blocks(): lax.all_to_all(tiles, axes[k], split_axis=k, concat_axis=k, tiled=True)]
    dot_general x4 -> x0, matrix products: 16.1 us -> none  [the longest x1 11.6 us: shards(): upd = jnp.dot(act, w_out, preferred_element_type=jnp.float32)]
    all_to_all x1 -> x0, blocking collectives: 11.6 us -> none  [shards(): lax.all_to_all(scored, MEM, split_axis=0, concat_axis=2, tiled=True)[0]]
    convert_element_type x4 -> x0, other arithmetic: 9.28 us -> none  [the longest x1 4.84 us: shards(): latent = (fine_skip.astype(jnp.float32) + unpooled).astype(jnp.bfloat16)]
    add x16 -> x0, other arithmetic: 6.8 us -> none  [add_member(): return inner + slope(members_f - other, inv_sq)]
  transfers between devices with their start and end apart: 6 -> 0, of which waited for: 4 -> 0; matrix products, arithmetic and copies ran while one was open for 4% -> 0% of each run, Pallas kernels for 0% -> 0%
where the time goes in v1:
time: 115 us
  Pallas kernels  107 us (93%)
  local copies, waits for them, and re-layouts  3.43 us (3%)
  matrix products  3.04 us (3%)
  between operations  1.29 us (1%)
    pallas_call x1, Pallas kernels, shards(): pl.pallas_call(kernel, name='decoder_tail', out_shape=(jax.ShapeDtypeStru...  107 us
    unnamed x4, local copies, waits for them, and re-layouts  3.43 us
    dot_general x1, matrix products, shards(): lax.dot_general(gscore, w_head, (((0,), (1,)), ((), ())), preferred_eleme...  3.04 us

profile of v1, /device:TPU:8, one launch (start us, length us, event | category | flops | bytes accessed | tf_op | source)
XLA Modules:
  0.0 114.6 jit_solution(1453011150356118027)
XLA Ops:
  1.3 1.7 %copy.16.w_head = bf16[512,83]{1,0:T(8,128)(2,1)} copy(bf16[512,83]{0,1:T(8,128)(2,1)} %param.27) | data formatting | bytes 169984 | tf_op args[13]
  2.9 0.0 copy-start
  2.9 106.8 %decoder_tail.1 = (bf16[83,2048]{1,0:T(8,128)(2,1)}, f32[83,512]{1,0:T(8,128)}) custom-call(bf16[512,512]{1,0:T(8,128)(2,1)} %bitcast.12, s32[16,128]{1,0:T(8,128)} %bitcast.14, s32[3,2048]{1,0:T(4,128)} %up_index.1, f32[3,2048]{1,0:T(4,128)} %up_weight.1, s32[6,2048]{1,0:T(8,128)} %neighbors.1, s32[1]{0:T(128)S(6)} %copy.18.live, f32[1,2048]{1,0:T(1,128)} %bitcast.15, ...), custom_call_target="tpu_custom_call" | custom-call | tf_op jit(solution)/shard_map/decoder_tail/pallas_call | solution.py:524
  109.8 1.8 %copy.17 = f32[1,512,83]{1,0,2:T(1,128)} copy(f32[1,512,83]{1,2,0:T(8,128)} %bitcast.13) | data formatting | bytes 339968
  111.6 0.0 copy-done
  111.6 3.0 %fusion = bf16[1,2048,512]{2,1,0:T(8,128)(2,1)} fusion(bf16[83,2048]{1,0:T(8,128)(2,1)} %get-tuple-element.4, bf16[512,83]{0,1:T(8,128)(2,1)S(1)} %copy-done), kind=kOutput, calls=%fused_computation.1 | convolution fusion | flops 175112192 | bytes 2522112 | tf_op jit(solution)/shard_map/dot_general | solution.py:600
Async XLA Ops:
  2.9 108.6 %copy-start = (bf16[512,83]{0,1:T(8,128)(2,1)S(1)}, bf16[512,83]{0,1:T(8,128)(2,1)}, u32[]{:S(2)}) copy-start(bf16[512,83]{0,1:T(8,128)(2,1)} %param.27) | copy-start | bytes 254980

commit v2 on v1

--- a/solution.py
+++ b/solution.py
@@ -50,7 +50,6 @@
     hidden,
     win,
     wout,
-    whp,
     wht,
     kwp,
     inv_b,
@@ -60,6 +59,7 @@
     pf,
     ssend,
     gs,
+    gst,
     hp,
     hr,
     hs,
@@ -221,10 +221,8 @@
         lax.fori_loop(0, 4, part, 0)
         return carry
 
-    whp[...] = jnp.zeros((512, 128), F32)
-    whp[:, :VARS] = w_head[...].astype(F32)
-    for q in range(4):
-        wht[:, q * 128 : q * 128 + 128] = whp[q * 128 : q * 128 + 128, :].T[:VP].astype(BF16)
+    wht[...] = jnp.zeros((VP, 512), BF16)
+    wht[:VARS, :] = w_head[...]
     kwp[...] = jnp.ones((8, 128), F32)
     kwp[0:1, :VARS] = kwidth[...]
     width = kwp[0:1, :]
@@ -270,36 +268,39 @@
             sibbuf.at[0], recv.at[rel, half], sib_s.at[0], recv_sem.at[rel, kb], dom=c * 2 + other
         ).wait_recv()
 
-    def added(rel, t, first):
-        at = pl.ds(pl.multiple_of(t * 256, 256), 256)
-        table = recv[rel]
-        here = chip(rel)
-        total = jnp.dot(wbuf[here, at, :256], table, preferred_element_type=F32)
-        total = total + jnp.dot(wbuf[here, at, 256:], table, preferred_element_type=F32)
-        before = skipv[at, :].astype(F32) if first else acc[at, :]
-        return at, before + total
-
-    for rel in (0, 7, 1, 6, 2, 5, 3):
-        arrived(rel, other)
-        if rel not in (0, 7, 1):
-            arrived(rel, k)
-
-        def accumulate(t, carry, rel=rel):
-            at, total = added(rel, t, rel == 0)
+    def added(rels, t):
+        at = pl.ds(pl.multiple_of(t * 512, 512), 512)
+        total = skipv[at, :].astype(F32) if rels == (0,) else acc[at, :]
+        for rel in rels:
+            here = chip(rel)
+            table = recv[rel]
+            total = total + jnp.dot(wbuf[here, at, :256], table, preferred_element_type=F32)
+            total = total + jnp.dot(wbuf[here, at, 256:], table, preferred_element_type=F32)
+        return at, total
+
+    for rels in ((0,), (7, 1), (4,), (5, 3)):
+        for rel in rels:
+            arrived(rel, other)
+            if rel not in (0, 7, 1):
+                arrived(rel, k)
+
+        def accumulate(t, carry, rels=rels):
+            at, total = added(rels, t)
             acc[at, :] = total
             return carry
 
-        lax.fori_loop(0, 8, accumulate, 0)
-
-    arrived(4, 0)
-    arrived(4, 1)
+        lax.fori_loop(0, 4, accumulate, 0)
+
+    for rel in (6, 2):
+        arrived(rel, 0)
+        arrived(rel, 1)
 
     def finish(t, carry):
-        at, total = added(4, t, False)
-        ext[pl.ds(pl.multiple_of(t * 256 + 128, 128), 256), :] = total.astype(BF16)
-        return carry
-
-    lax.fori_loop(0, 2, lambda t, carry: finish(t * 7, carry), 0)
+        total = added((6, 2), t)[1]
+        ext[pl.ds(pl.multiple_of(t * 512 + 128, 128), 512), :] = total.astype(BF16)
+        return carry
+
+    lax.fori_loop(0, 2, lambda t, carry: finish(t * 3, carry), 0)
     rims = [
         remote(
             ext.at[pl.ds(2048, 128)],
@@ -318,7 +319,7 @@
     ]
     for rim in rims:
         rim.start()
-    lax.fori_loop(1, 7, finish, 0)
+    lax.fori_loop(1, 3, finish, 0)
     loads[2].wait()
     loads[3].wait()
 
@@ -329,14 +330,15 @@
         return r, remote(psend.at[j], pall.at[r], pred_s.at[r], pred_r.at[r], mem=j)
 
     def dense(i, carry):
-        at = pl.ds(pl.multiple_of(i * 256 + 128, 128), 256)
-        x = ext[at, :]
-        total = jnp.dot(
-            nbuf[pl.ds(pl.multiple_of(i * 256, 256), 256), :],
-            ext[pl.ds(pl.multiple_of(i * 256, 256), 512), :],
-            preferred_element_type=F32,
-        )
-        agg = (total / 6.0).astype(BF16)
+        x = ext[pl.ds(pl.multiple_of(i * 512 + 128, 128), 512), :]
+        parts = []
+        for s in range(2):
+            start = pl.multiple_of(i * 512 + s * 256, 256)
+            total = jnp.dot(
+                nbuf[pl.ds(start, 256), :], ext[pl.ds(start, 512), :], preferred_element_type=F32
+            )
+            parts.append((total * (1.0 / 6)).astype(BF16))
+        agg = jnp.concatenate(parts, axis=0)
         pre = jnp.dot(x, win[:512], preferred_element_type=F32) + jnp.dot(
             agg, win[512:], preferred_element_type=F32
         )
@@ -347,10 +349,10 @@
         centred = upd - mean
         var = jnp.sum(centred * centred, axis=1, keepdims=True) * (1.0 / 512)
         h = (x.astype(F32) + centred * lax.rsqrt(var + 1e-05) * gain_row).astype(BF16)
-        hidden[pl.ds(pl.multiple_of(i * 256, 256), 256), :] = h
+        hidden[pl.ds(pl.multiple_of(i * 512, 512), 512), :] = h
         pred = lax.dot_general(wht[...], h, NT, preferred_element_type=F32).astype(BF16)
-        for s in range(2):
-            j = 2 * i + s
+        for s in range(4):
+            j = 4 * i + s
             r, copy = pred_copy(j)
             psend[j] = pred[:, s * 128 : s * 128 + 128]
 
@@ -364,7 +366,7 @@
 
         return carry
 
-    lax.fori_loop(1, 7, dense, 0)
+    lax.fori_loop(1, 3, dense, 0)
     for rim in rims:
         rim.wait()
 
@@ -376,7 +378,7 @@
     def _():
         ext[pl.ds(2176, 128), :] = jnp.zeros((128, 512), BF16)
 
-    lax.fori_loop(0, 2, lambda t, carry: dense(t * 7, carry), 0)
+    lax.fori_loop(0, 2, lambda t, carry: dense(t * 3, carry), 0)
 
     def pred_wait(r, carry):
         remote(psend.at[0], pall.at[r], pred_s.at[r], pred_r.at[r], mem=member(r)).wait_recv()
@@ -444,7 +446,15 @@
 
     lax.fori_loop(1, 16, spread, 0)
     hr[0] = hp[me_m]
-    gs_out[...] = gs[:VARS, :]
+
+    def turn(j, carry):
+        at = pl.ds(pl.multiple_of(j * 128, 128), 128)
+        gst[at, :] = gs[:, at].astype(F32).T[:, :VARS].astype(BF16)
+        return carry
+
+    lax.fori_loop(0, 16, turn, 0)
+    turned = pltpu.make_async_copy(gst, gs_out, loc_sem.at[4])
+    turned.start()
 
     def hr_wait(r, carry):
         hr_copy(r).wait_recv()
@@ -475,8 +485,9 @@
     for j in range(16):
         lo = 24 * (j // 4)
         n = min(24, VARS - lo)
-        head_out[lo : lo + n, 128 * (j % 4) : 128 * (j % 4) + 128] = hall[j, :n]
-
+        head_out[lo : lo + n, 0, 128 * (j % 4) : 128 * (j % 4) + 128] = hall[j, :n]
+
+    turned.wait()
     for copy in to_right + to_left + sib_copies:
         copy.wait_send()
 
@@ -525,11 +536,11 @@
         kernel,
         name="decoder_tail",
         out_shape=(
-            jax.ShapeDtypeStruct((VARS, 2048), BF16),
-            jax.ShapeDtypeStruct((VARS, 512), F32),
+            jax.ShapeDtypeStruct((2048, VARS), BF16),
+            jax.ShapeDtypeStruct((VARS, 1, 512), F32),
         ),
         in_specs=[hbm, vmem, vmem, vmem, vmem, smem, vmem, hbm, vmem, vmem, hbm, hbm, vmem, vmem],
-        out_specs=(vmem, vmem),
+        out_specs=(hbm, vmem),
         scratch_shapes=[
             pltpu.VMEM((3, 512, 512), BF16),
             pltpu.VMEM((2, 16, 128), jnp.int32),
@@ -545,7 +556,6 @@
             pltpu.VMEM((2048, 512), BF16),
             pltpu.VMEM((1024, 512), BF16),
             pltpu.VMEM((512, 512), BF16),
-            pltpu.VMEM((512, 128), F32),
             pltpu.VMEM((VP, 512), BF16),
             pltpu.VMEM((8, 128), F32),
             pltpu.VMEM((VP, 128), F32),
@@ -555,11 +565,12 @@
             pltpu.VMEM((16, VP, 128), F32),
             pltpu.VMEM((16, VP, 128), BF16),
             pltpu.VMEM((VP, 2048), BF16),
+            pltpu.VMEM((2048, VARS), BF16),
             pltpu.VMEM((16, 24, 128), F32),
             pltpu.VMEM((16, 24, 128), F32),
             pltpu.VMEM((24, 128), F32),
             pltpu.VMEM((16, 24, 128), F32),
-            dma((4,)),
+            dma((5,)),
             dma((2,)),
             dma((2,)),
             dma((2,)),
@@ -595,12 +606,12 @@
         w_in,
         w_out,
         ln_gain[None],
-        w_head,
+        w_head.T,
     )
     grad_latent = lax.dot_general(
-        gscore, w_head, (((0,), (1,)), ((), ())), preferred_element_type=F32
+        gscore, w_head, (((1,), (1,)), ((), ())), preferred_element_type=F32
     ).astype(BF16)
-    return grad_latent[None], head.T[None]
+    return grad_latent[None], head.transpose(1, 2, 0)
 
 
 def solution(mesh):

time: 115 us -> 99.4 us (0.86)
  Pallas kernels: 107 us -> 92.8 us
  local copies, waits for them, and re-layouts: 3.43 us -> 0.68 us
    pallas_call x1, Pallas kernels: 107 us -> 92.8 us  [shards(): pl.pallas_call(kernel, name='decoder_tail', out_shape=(jax.ShapeDtypeStru...]
    unnamed x4 -> x5, local copies, waits for them, and re-layouts: 3.43 us -> 0.68 us
where the time goes in v2:
time: 99.4 us; the launch traced here: 97.9 us
  Pallas kernels  92.8 us (93%)
  matrix products  3.08 us (3%)
  between operations  1.31 us (1%)
    pallas_call x1, Pallas kernels, shards(): pl.pallas_call(kernel, name='decoder_tail', out_shape=(jax.ShapeDtypeStru...  92.8 us
    dot_general x1, matrix products, shards(): lax.dot_general(gscore, w_head, (((1,), (1,)), ((), ())), preferred_eleme...  3.08 us

profile of v2, /device:TPU:8, one launch (start us, length us, event | category | flops | bytes accessed | tf_op | source)
XLA Modules:
  0.0 97.9 jit_solution(6298627388349429486)
XLA Ops:
  1.3 0.0 copy-start
  1.3 92.8 %decoder_tail.1 = (bf16[2048,83]{1,0:T(8,128)(2,1)}, f32[83,1,512]{2,1,0:T(1,128)}) custom-call(bf16[512,512]{1,0:T(8,128)(2,1)} %bitcast.11, s32[16,128]{1,0:T(8,128)} %bitcast.14, s32[3,2048]{1,0:T(4,128)} %up_index.1, f32[3,2048]{1,0:T(4,128)} %up_weight.1, s32[6,2048]{1,0:T(8,128)} %neighbors.1, s32[1]{0:T(128)S(6)} %copy.17.live, f32[1,2048]{1,0:T(1,128)} %bitcast.15, ...), custom_call_target="tpu_custom_call" | custom-call | tf_op jit(solution)/shard_map/decoder_tail/pallas_call | solution.py:535
  94.1 0.0 copy-start.1
  94.1 0.0 copy-done
  94.2 3.1 %fusion = bf16[1,2048,512]{2,1,0:T(8,128)(2,1)} fusion(bf16[2048,83]{1,0:T(8,128)(2,1)} %get-tuple-element.4, bf16[512,83]{0,1:T(8,128)(2,1)S(1)} %copy-done), kind=kOutput, calls=%fused_computation.1 | convolution fusion | flops 175112192 | bytes 2522112 | tf_op jit(solution)/shard_map/dot_general | solution.py:611
  97.2 0.0 copy-done.1
  97.2 0.7 copy.18
Async XLA Ops:
  1.3 92.9 %copy-start = (bf16[512,83]{0,1:T(8,128)(2,1)S(1)}, bf16[512,83]{0,1:T(8,128)(2,1)}, u32[]{:S(2)}) copy-start(bf16[512,83]{0,1:T(8,128)(2,1)} %param.27) | copy-start | bytes 254980
  94.1 3.1 %copy-start.1 = (f32[83,1,512]{2,1,0:T(1,128)S(1)}, f32[83,1,512]{2,1,0:T(1,128)}, u32[]{:S(2)}) copy-start(f32[83,1,512]{2,1,0:T(1,128)} %get-tuple-element.5) | copy-start | bytes 509956

commit v3 on v2

--- a/solution.py
+++ b/solution.py
@@ -45,6 +45,7 @@
     sbuf,
     sibbuf,
     acc,
+    part,
     skipv,
     ext,
     hidden,
@@ -121,24 +122,34 @@
 
     lax.fori_loop(1, 16, greet, 0)
     loads = [
-        pltpu.make_async_copy(coarse, tiles.at[0], loc_sem.at[0]),
+        pltpu.make_async_copy(coarse.at[:, :256], tiles.at[0, 0], loc_sem.at[0]),
         pltpu.make_async_copy(skip, skipv, loc_sem.at[1]),
         pltpu.make_async_copy(w_in, win, loc_sem.at[2]),
         pltpu.make_async_copy(w_out, wout, loc_sem.at[3]),
+        pltpu.make_async_copy(coarse.at[:, 256:], tiles.at[1, 0], loc_sem.at[4]),
     ]
     for load in loads:
         load.start()
     pl.semaphore_wait(barrier, 30)
 
-    to_right = [
-        remote(coarse, tiles.at[1], tile_s.at[0], tile_r.at[0], dom=chip(1) * 2 + k),
-        remote(send_rows, rows.at[0], rows_s.at[0], rows_r.at[0], dom=chip(1) * 2 + k),
+    next_to = (chip(1) * 2 + k, chip(-1) * 2 + k)
+    row_copies = [
+        remote(send_rows, rows.at[i], rows_s.at[i], rows_r.at[i], dom=next_to[i]) for i in range(2)
     ]
-    to_left = [
-        remote(coarse, tiles.at[2], tile_s.at[1], tile_r.at[1], dom=chip(-1) * 2 + k),
-        remote(send_rows, rows.at[1], rows_s.at[1], rows_r.at[1], dom=chip(-1) * 2 + k),
+    tile_copies = [
+        [
+            remote(
+                coarse.at[:, 256 * h : 256 * h + 256],
+                tiles.at[h, 1 + i],
+                tile_s.at[h, i],
+                tile_r.at[h, i],
+                dom=next_to[i],
+            )
+            for i in range(2)
+        ]
+        for h in range(2)
     ]
-    for copy in to_right + to_left:
+    for copy in row_copies + tile_copies[0] + tile_copies[1]:
         copy.start()
 
     lane = lax.broadcasted_iota(jnp.int32, (128, 128), 1).astype(F32)
@@ -153,21 +164,23 @@
 
     my_rows = pl.ds(pl.multiple_of(k * 128, 128), 128)
 
-    def at_home(table, tile, slot, rel):
-        sibbuf[slot] = picked(table, tile, me_d + other - k)
+    def at_home(h, table, slot, rel):
+        tile = tiles.at[h, slot]
+        sibbuf[h, slot] = picked(table, tile, me_d + other - k)
         copy = remote(
-            sibbuf.at[slot],
-            recv.at[rel, my_rows],
-            sib_s.at[slot],
-            recv_sem.at[rel, k],
+            sibbuf.at[h, slot],
+            recv.at[h, rel, my_rows],
+            sib_s.at[h, slot],
+            recv_sem.at[h, rel, k],
             dom=c * 2 + other,
         )
         copy.start()
-        recv[rel, my_rows, :] = picked(table, tile, me_d)
+        recv[h, rel, my_rows, :] = picked(table, tile, me_d)
         return copy
 
     loads[0].wait()
-    sib_copies = [at_home(send_rows, tiles.at[0], 0, 0)]
+    loads[4].wait()
+    sib_copies = [at_home(0, send_rows, 0, 0), at_home(1, send_rows, 0, 0)]
 
     def weights_of(t, carry):
         at = pl.ds(pl.multiple_of(t * 128, 128), 128)
@@ -175,7 +188,7 @@
             cols[j] = lanes_of(up_index[j : j + 1, at].astype(F32))
             cols[3 + j] = lanes_of(up_weight[j : j + 1, at])
 
-        def part(s, carry):
+        def rows_of(s, carry):
             sub = pl.ds(pl.multiple_of(s * 32, 32), 32)
             out = pl.ds(pl.multiple_of(t * 128 + s * 32, 32), 32)
             idx = [cols[j, sub, :] for j in range(3)]
@@ -194,10 +207,8 @@
                 wbuf[q // 2, out, 256 + (q % 2) * 128 : 384 + (q % 2) * 128] = lo
             return carry
 
-        lax.fori_loop(0, 4, part, 0)
-        return carry
-
-    lax.fori_loop(0, 16, weights_of, 0)
+        lax.fori_loop(0, 4, rows_of, 0)
+        return carry
 
     def counts_of(t, carry):
         at = pl.ds(pl.multiple_of(t * 128, 128), 128)
@@ -205,7 +216,7 @@
         for j in range(6):
             cols[j] = lanes_of(neighbors[j : j + 1, at].astype(F32) - shift)
 
-        def part(s, carry):
+        def rows_of(s, carry):
             sub = pl.ds(pl.multiple_of(s * 32, 32), 32)
             out = pl.ds(pl.multiple_of(t * 128 + s * 32, 32), 32)
             idx = [cols[j, sub, :] for j in range(6)]
@@ -218,7 +229,7 @@
                 nbuf[out, q * 128 : q * 128 + 128] = total.astype(BF16)
             return carry
 
-        lax.fori_loop(0, 4, part, 0)
+        lax.fori_loop(0, 4, rows_of, 0)
         return carry
 
     wht[...] = jnp.zeros((VP, 512), BF16)
@@ -233,115 +244,161 @@
 
     lax.fori_loop(0, 16, counts_of, 0)
 
-    for copy in to_right + to_left:
-        copy.wait_recv()
-
-    def far_copy(side, j, o, kd):
+    def far_copy(h, side, j, o, kd):
         dest = chip(o) * 2 + kd
         rel = 4 + (j + 1) // 2 if side == 0 else 4 - (j + 1) // 2
         return dest, remote(
-            sbuf.at[side, j],
-            recv.at[rel, my_rows],
-            g_s.at[side, j],
-            recv_sem.at[rel, k],
+            sbuf.at[h, side, j],
+            recv.at[h, rel, my_rows],
+            g_s.at[h, side, j],
+            recv_sem.at[h, rel, k],
             dom=dest,
         )
 
-    def both_ways(j, carry):
-        o = 3 - (j + 1) // 2
-        even = lax.rem(j, 2)
-        for side in range(2):
-            dest, copy = far_copy(side, j, o if side == 0 else -o, even if side == 0 else 1 - even)
-            sbuf[side, j] = picked(rows.at[side], tiles.at[1 + side], dest)
-            copy.start()
-        return carry
-
-    lax.fori_loop(0, 5, both_ways, 0)
-    sib_copies.append(at_home(rows.at[0], tiles.at[1], 1, 7))
-    sib_copies.append(at_home(rows.at[1], tiles.at[2], 2, 1))
-
-    loads[1].wait()
-
-    def arrived(rel, kb):
+    def send_on(h):
+        for copy in tile_copies[h]:
+            copy.wait_recv()
+
+        def both_ways(j, carry):
+            o = 3 - (j + 1) // 2
+            even = lax.rem(j, 2)
+            for side in range(2):
+                dest, copy = far_copy(
+                    h, side, j, o if side == 0 else -o, even if side == 0 else 1 - even
+                )
+                sbuf[h, side, j] = picked(rows.at[side], tiles.at[h, 1 + side], dest)
+                copy.start()
+            return carry
+
+        lax.fori_loop(0, 5, both_ways, 0)
+        sib_copies.append(at_home(h, rows.at[0], 1, 7))
+        sib_copies.append(at_home(h, rows.at[1], 2, 1))
+
+    for copy in row_copies:
+        copy.wait_recv()
+    send_on(0)
+    lax.fori_loop(0, 16, weights_of, 0)
+    send_on(1)
+    for load in loads[1:4]:
+        load.wait()
+
+    def arrived(h, rel, kb):
         half = pl.ds(pl.multiple_of(kb * 128, 128), 128)
         remote(
-            sibbuf.at[0], recv.at[rel, half], sib_s.at[0], recv_sem.at[rel, kb], dom=c * 2 + other
+            sibbuf.at[h, 0],
+            recv.at[h, rel, half],
+            sib_s.at[h, 0],
+            recv_sem.at[h, rel, kb],
+            dom=c * 2 + other,
         ).wait_recv()
 
-    def added(rels, t):
-        at = pl.ds(pl.multiple_of(t * 512, 512), 512)
-        total = skipv[at, :].astype(F32) if rels == (0,) else acc[at, :]
-        for rel in rels:
-            here = chip(rel)
-            table = recv[rel]
-            total = total + jnp.dot(wbuf[here, at, :256], table, preferred_element_type=F32)
-            total = total + jnp.dot(wbuf[here, at, 256:], table, preferred_element_type=F32)
-        return at, total
-
-    for rels in ((0,), (7, 1), (4,), (5, 3)):
-        for rel in rels:
-            arrived(rel, other)
-            if rel not in (0, 7, 1):
-                arrived(rel, k)
-
-        def accumulate(t, carry, rels=rels):
-            at, total = added(rels, t)
-            acc[at, :] = total
+    def unpooled(h):
+        mine = slice(256 * h, 256 * h + 256)
+
+        def added(rels, t):
+            at = pl.ds(pl.multiple_of(t * 512, 512), 512)
+            total = skipv[at, mine].astype(F32) if rels == (0,) else acc[at, :]
+            for rel in rels:
+                here = chip(rel)
+                table = recv[h, rel]
+                total = total + jnp.dot(wbuf[here, at, :256], table, preferred_element_type=F32)
+                total = total + jnp.dot(wbuf[here, at, 256:], table, preferred_element_type=F32)
+            return at, total
+
+        for rels in ((0,), (7, 1), (4,), (5, 3)):
+            for rel in rels:
+                arrived(h, rel, other)
+                if rel not in (0, 7, 1):
+                    arrived(h, rel, k)
+
+            def accumulate(t, carry, rels=rels):
+                at, total = added(rels, t)
+                acc[at, :] = total
+                return carry
+
+            lax.fori_loop(0, 4, accumulate, 0)
+
+        for rel in (6, 2):
+            arrived(h, rel, 0)
+            arrived(h, rel, 1)
+
+        def finish(t, carry):
+            total = added((6, 2), t)[1]
+            ext[h, pl.ds(pl.multiple_of(t * 512 + 128, 128), 512), :] = total.astype(BF16)
             return carry
 
-        lax.fori_loop(0, 4, accumulate, 0)
-
-    for rel in (6, 2):
-        arrived(rel, 0)
-        arrived(rel, 1)
-
-    def finish(t, carry):
-        total = added((6, 2), t)[1]
-        ext[pl.ds(pl.multiple_of(t * 512 + 128, 128), 512), :] = total.astype(BF16)
-        return carry
-
-    lax.fori_loop(0, 2, lambda t, carry: finish(t * 3, carry), 0)
-    rims = [
-        remote(
-            ext.at[pl.ds(2048, 128)],
-            ext.at[pl.ds(0, 128)],
-            rim_s.at[0],
-            rim_r.at[0],
-            dom=lax.rem(me_d + 1, 16),
-        ),
-        remote(
-            ext.at[pl.ds(128, 128)],
-            ext.at[pl.ds(2176, 128)],
-            rim_s.at[1],
-            rim_r.at[1],
-            dom=lax.rem(me_d + 15, 16),
-        ),
-    ]
-    for rim in rims:
-        rim.start()
-    lax.fori_loop(1, 3, finish, 0)
-    loads[2].wait()
-    loads[3].wait()
-
-    gain_row = gain[...]
-
-    def pred_copy(j):
-        r = lax.rem(j - me_m + 16, 16)
-        return r, remote(psend.at[j], pall.at[r], pred_s.at[r], pred_r.at[r], mem=j)
-
-    def dense(i, carry):
-        x = ext[pl.ds(pl.multiple_of(i * 512 + 128, 128), 512), :]
+        lax.fori_loop(0, 2, lambda t, carry: finish(t * 3, carry), 0)
+        rims = [
+            remote(
+                ext.at[h, pl.ds(2048, 128)],
+                ext.at[h, pl.ds(0, 128)],
+                rim_s.at[h, 0],
+                rim_r.at[h, 0],
+                dom=lax.rem(me_d + 1, 16),
+            ),
+            remote(
+                ext.at[h, pl.ds(128, 128)],
+                ext.at[h, pl.ds(2176, 128)],
+                rim_s.at[h, 1],
+                rim_r.at[h, 1],
+                dom=lax.rem(me_d + 15, 16),
+            ),
+        ]
+        for rim in rims:
+            rim.start()
+        lax.fori_loop(1, 3, finish, 0)
+        return rims
+
+    def rims_done(h, rims):
+        for rim in rims:
+            rim.wait()
+
+        @pl.when(me_d == 0)
+        def _():
+            ext[h, pl.ds(0, 128), :] = jnp.zeros((128, 256), BF16)
+
+        @pl.when(me_d == 15)
+        def _():
+            ext[h, pl.ds(2176, 128), :] = jnp.zeros((128, 256), BF16)
+
+    def half_pre(h, i):
+        x = ext[h, pl.ds(pl.multiple_of(i * 512 + 128, 128), 512), :]
         parts = []
         for s in range(2):
             start = pl.multiple_of(i * 512 + s * 256, 256)
             total = jnp.dot(
-                nbuf[pl.ds(start, 256), :], ext[pl.ds(start, 512), :], preferred_element_type=F32
+                nbuf[pl.ds(start, 256), :],
+                ext[h, pl.ds(start, 512), :],
+                preferred_element_type=F32,
             )
             parts.append((total * (1.0 / 6)).astype(BF16))
         agg = jnp.concatenate(parts, axis=0)
-        pre = jnp.dot(x, win[:512], preferred_element_type=F32) + jnp.dot(
-            agg, win[512:], preferred_element_type=F32
+        lo = 256 * h
+        return x, jnp.dot(x, win[lo : lo + 256], preferred_element_type=F32) + jnp.dot(
+            agg, win[512 + lo : 768 + lo], preferred_element_type=F32
         )
+
+    def begin(i, carry):
+        part[pl.ds(pl.multiple_of(i * 512, 512), 512), :] = half_pre(0, i)[1]
+        return carry
+
+    first_rims = unpooled(0)
+    lax.fori_loop(1, 3, begin, 0)
+    rims_done(0, first_rims)
+    lax.fori_loop(0, 2, lambda t, carry: begin(t * 3, carry), 0)
+    rims = unpooled(1)
+
+    gain_row = gain[...]
+
+    def pred_copy(j):
+        r = lax.rem(j - me_m + 16, 16)
+        return r, remote(psend.at[j], pall.at[r], pred_s.at[r], pred_r.at[r], mem=j)
+
+    def dense(i, carry):
+        late, pre = half_pre(1, i)
+        pre = pre + part[pl.ds(pl.multiple_of(i * 512, 512), 512), :]
+        early = ext[0, pl.ds(pl.multiple_of(i * 512 + 128, 128), 512), :]
+        x = jnp.concatenate([early, late], axis=1)
         half = 0.5 * pre
         act = (half + half * jnp.tanh(half)).astype(BF16)
         upd = jnp.dot(act, wout[...], preferred_element_type=F32)
@@ -367,17 +424,7 @@
         return carry
 
     lax.fori_loop(1, 3, dense, 0)
-    for rim in rims:
-        rim.wait()
-
-    @pl.when(me_d == 0)
-    def _():
-        ext[pl.ds(0, 128), :] = jnp.zeros((128, 512), BF16)
-
-    @pl.when(me_d == 15)
-    def _():
-        ext[pl.ds(2176, 128), :] = jnp.zeros((128, 512), BF16)
-
+    rims_done(1, rims)
     lax.fori_loop(0, 2, lambda t, carry: dense(t * 3, carry), 0)
 
     def pred_wait(r, carry):
@@ -435,7 +482,8 @@
 
     head = jnp.dot(gs[...], hidden[...], preferred_element_type=F32)
     for j in range(16):
-        hp[j] = head[24 * (j // 4) : 24 * (j // 4) + 24, 128 * (j % 4) : 128 * (j % 4) + 128]
+        lo, left = 24 * (j // 4), 128 * (j % 4)
+        hp[j] = head[lo : lo + 24, left : left + 128].astype(BF16)
 
     def hr_copy(r):
         return remote(hp.at[member(r)], hr.at[r], hr_s.at[r], hr_r.at[r], mem=member(r))
@@ -453,7 +501,7 @@
         return carry
 
     lax.fori_loop(0, 16, turn, 0)
-    turned = pltpu.make_async_copy(gst, gs_out, loc_sem.at[4])
+    turned = pltpu.make_async_copy(gst, gs_out, loc_sem.at[5])
     turned.start()
 
     def hr_wait(r, carry):
@@ -461,10 +509,10 @@
         return carry
 
     lax.fori_loop(1, 16, hr_wait, 0)
-    summed = hr[0]
+    summed = hr[0].astype(F32)
     for r in range(1, 16):
-        summed = summed + hr[r]
-    summed = summed * (1.0 / math.sqrt(32768))
+        summed = summed + hr[r].astype(F32)
+    summed = (summed * (1.0 / math.sqrt(32768))).astype(BF16)
     hs[...] = summed
     hall[me_m] = summed
 
@@ -485,19 +533,20 @@
     for j in range(16):
         lo = 24 * (j // 4)
         n = min(24, VARS - lo)
-        head_out[lo : lo + n, 0, 128 * (j % 4) : 128 * (j % 4) + 128] = hall[j, :n]
+        head_out[lo : lo + n, 0, 128 * (j % 4) : 128 * (j % 4) + 128] = hall[j].astype(F32)[:n]
 
     turned.wait()
-    for copy in to_right + to_left + sib_copies:
+    for copy in row_copies + tile_copies[0] + tile_copies[1] + sib_copies:
         copy.wait_send()
 
     def far_done(j, carry):
         o = 3 - (j + 1) // 2
         even = lax.rem(j, 2)
-        for side in range(2):
-            far_copy(side, j, o if side == 0 else -o, even if side == 0 else 1 - even)[
-                1
-            ].wait_send()
+        for h in range(2):
+            for side in range(2):
+                far_copy(h, side, j, o if side == 0 else -o, even if side == 0 else 1 - even)[
+                    1
+                ].wait_send()
         return carry
 
     lax.fori_loop(0, 5, far_done, 0)
@@ -510,6 +559,10 @@
         return carry
 
     lax.fori_loop(1, 16, members_done, 0)
+
+
+def back(score, w_head, out):
+    out[...] = jnp.dot(score[...], w_head[...], preferred_element_type=F32).astype(BF16)
 
 
 def shards(
@@ -542,17 +595,18 @@
         in_specs=[hbm, vmem, vmem, vmem, vmem, smem, vmem, hbm, vmem, vmem, hbm, hbm, vmem, vmem],
         out_specs=(hbm, vmem),
         scratch_shapes=[
-            pltpu.VMEM((3, 512, 512), BF16),
+            pltpu.VMEM((2, 3, 512, 256), BF16),
             pltpu.VMEM((2, 16, 128), jnp.int32),
             pltpu.VMEM((8, 2048, 512), BF16),
             pltpu.VMEM((2048, 512), BF16),
             pltpu.VMEM((6, 128, 128), F32),
-            pltpu.VMEM((8, 256, 512), BF16),
-            pltpu.VMEM((2, 5, 128, 512), BF16),
-            pltpu.VMEM((3, 128, 512), BF16),
+            pltpu.VMEM((2, 8, 256, 256), BF16),
+            pltpu.VMEM((2, 2, 5, 128, 256), BF16),
+            pltpu.VMEM((2, 3, 128, 256), BF16),
+            pltpu.VMEM((2048, 256), F32),
             pltpu.VMEM((2048, 512), F32),
             pltpu.VMEM((2048, 512), BF16),
-            pltpu.VMEM((2304, 512), BF16),
+            pltpu.VMEM((2, 2304, 256), BF16),
             pltpu.VMEM((2048, 512), BF16),
             pltpu.VMEM((1024, 512), BF16),
             pltpu.VMEM((512, 512), BF16),
@@ -566,20 +620,20 @@
             pltpu.VMEM((16, VP, 128), BF16),
             pltpu.VMEM((VP, 2048), BF16),
             pltpu.VMEM((2048, VARS), BF16),
-            pltpu.VMEM((16, 24, 128), F32),
-            pltpu.VMEM((16, 24, 128), F32),
-            pltpu.VMEM((24, 128), F32),
-            pltpu.VMEM((16, 24, 128), F32),
-            dma((5,)),
+            pltpu.VMEM((16, 24, 128), BF16),
+            pltpu.VMEM((16, 24, 128), BF16),
+            pltpu.VMEM((24, 128), BF16),
+            pltpu.VMEM((16, 24, 128), BF16),
+            dma((6,)),
+            dma((2, 2)),
+            dma((2, 2)),
             dma((2,)),
             dma((2,)),
-            dma((2,)),
-            dma((2,)),
-            dma((2, 5)),
-            dma((3,)),
-            dma((8, 2)),
-            dma((2,)),
-            dma((2,)),
+            dma((2, 2, 5)),
+            dma((2, 3)),
+            dma((2, 8, 2)),
+            dma((2, 2)),
+            dma((2, 2)),
             dma((16,)),
             dma((16,)),
             dma((16,)),
@@ -608,9 +662,17 @@
         ln_gain[None],
         w_head.T,
     )
-    grad_latent = lax.dot_general(
-        gscore, w_head, (((1,), (1,)), ((), ())), preferred_element_type=F32
-    ).astype(BF16)
+    grad_latent = pl.pallas_call(
+        back,
+        name="latent_gradient",
+        out_shape=jax.ShapeDtypeStruct((2048, 512), BF16),
+        grid=(4,),
+        in_specs=[
+            pl.BlockSpec((512, VARS), lambda i: (i, 0)),
+            pl.BlockSpec((VARS, 512), lambda i: (0, 0)),
+        ],
+        out_specs=pl.BlockSpec((512, 512), lambda i: (i, 0)),
+    )(gscore, w_head.T)
     return grad_latent[None], head.transpose(1, 2, 0)
 
 

time: 99.4 us -> 99.4 us (level); the launches traced: 97.9 us -> 99.3 us
  Pallas kernels: 92.8 us -> 97.3 us
  matrix products: 3.08 us -> 0 us
    pallas_call x0 -> x1, Pallas kernels: none -> 4.05 us  [shards(): pl.pallas_call(back, name='latent_gradient', out_shape=jax.ShapeDtypeStru...]
    dot_general x1 -> x0, matrix products: 3.08 us -> none  [shards(): lax.dot_general(gscore, w_head, (((1,), (1,)), ((), ())), preferred_eleme...]
where the time goes in v3:
time: 99.4 us; the launch traced here: 99.3 us
  Pallas kernels  97.3 us (98%)
  between operations  1.3 us (1%)
    pallas_call x1, Pallas kernels, shards(): pl.pallas_call(kernel, name='decoder_tail', out_shape=(jax.ShapeDtypeStru...  93.2 us
    pallas_call x1, Pallas kernels, shards(): pl.pallas_call(back, name='latent_gradient', out_shape=jax.ShapeDtypeStru...  4.05 us

profile of v3, /device:TPU:8, one launch (start us, length us, event | category | flops | bytes accessed | tf_op | source)
XLA Modules:
  0.0 99.3 jit_solution(2432631731912164183)
XLA Ops:
  1.3 93.2 %decoder_tail.1 = (bf16[2048,83]{1,0:T(8,128)(2,1)}, f32[83,1,512]{2,1,0:T(1,128)}) custom-call(bf16[512,512]{1,0:T(8,128)(2,1)} %bitcast.9, s32[16,128]{1,0:T(8,128)} %bitcast.13, s32[3,2048]{1,0:T(4,128)} %up_index.1, f32[3,2048]{1,0:T(4,128)} %up_weight.1, s32[6,2048]{1,0:T(8,128)} %neighbors.1, s32[1]{0:T(128)S(6)} %copy.17.live, f32[1,2048]{1,0:T(1,128)} %bitcast.14, ...), custom_call_target="tpu_custom_call" | custom-call | tf_op jit(solution)/shard_map/decoder_tail/pallas_call | solution.py:588
  94.5 0.0 copy-start
  94.5 4.1 %latent_gradient.1 = bf16[2048,512]{1,0:T(8,128)(2,1)} custom-call(bf16[2048,83]{1,0:T(8,128)(2,1)} %get-tuple-element.4.score, bf16[83,512]{1,0:T(8,128)(2,1)} %bitcast.11), custom_call_target="tpu_custom_call" | custom-call | tf_op jit(solution)/shard_map/latent_gradient/pallas_call | solution.py:665
  98.6 0.0 copy-done
  98.6 0.7 copy.18
Async XLA Ops:
  94.5 4.1 %copy-start = (f32[83,1,512]{2,1,0:T(1,128)S(1)}, f32[83,1,512]{2,1,0:T(1,128)}, u32[]{:S(2)}) copy-start(f32[83,1,512]{2,1,0:T(1,128)} %get-tuple-element.5) | copy-start | bytes 509956

commit v4 on v2

--- a/solution.py
+++ b/solution.py
@@ -22,20 +22,29 @@
 def kernel(
     coarse,
     send_rows,
+    up_index_h,
+    up_weight_h,
+    neighbors_h,
+    live,
+    area_h,
+    skip,
+    targets_h,
+    kwidth_h,
+    w_in,
+    w_out,
+    gain_h,
+    w_head_h,
+    gs_out,
+    head_out,
+    own_rows,
     up_index,
     up_weight,
     neighbors,
-    live,
     area,
-    skip,
     targets,
     kwidth,
-    w_in,
-    w_out,
     gain,
     w_head,
-    gs_out,
-    head_out,
     tiles,
     rows,
     wbuf,
@@ -120,25 +129,61 @@
         return carry
 
     lax.fori_loop(1, 16, greet, 0)
+    my_share = pl.ds(pl.multiple_of(me_m * 128, 128), 128)
     loads = [
-        pltpu.make_async_copy(coarse, tiles.at[0], loc_sem.at[0]),
-        pltpu.make_async_copy(skip, skipv, loc_sem.at[1]),
-        pltpu.make_async_copy(w_in, win, loc_sem.at[2]),
-        pltpu.make_async_copy(w_out, wout, loc_sem.at[3]),
+        pltpu.make_async_copy(src, dst, loc_sem.at[i])
+        for i, (src, dst) in enumerate(
+            (
+                (send_rows, own_rows),
+                (coarse.at[:, :256], tiles.at[0, 0]),
+                (coarse.at[:, 256:], tiles.at[1, 0]),
+                (neighbors_h, neighbors),
+                (w_head_h, w_head),
+                (kwidth_h, kwidth),
+                (targets_h.at[:, my_share], targets),
+                (area_h.at[:, my_share], area),
+                (up_index_h, up_index),
+                (up_weight_h, up_weight),
+                (gain_h, gain),
+                (skip, skipv),
+                (w_in, win),
+                (w_out, wout),
+            )
+        )
     ]
     for load in loads:
         load.start()
     pl.semaphore_wait(barrier, 30)
 
-    to_right = [
-        remote(coarse, tiles.at[1], tile_s.at[0], tile_r.at[0], dom=chip(1) * 2 + k),
-        remote(send_rows, rows.at[0], rows_s.at[0], rows_r.at[0], dom=chip(1) * 2 + k),
+    next_to = (chip(1) * 2 + k, chip(-1) * 2 + k)
+
+    def pass_on(h, src, slot, side):
+        return remote(
+            src,
+            tiles.at[h, slot],
+            tile_s.at[h, slot - 1],
+            tile_r.at[h, slot - 1],
+            dom=next_to[side],
+        )
+
+    def pass_rows(src, slot, side):
+        return remote(
+            src,
+            rows.at[slot - 1],
+            rows_s.at[slot - 1],
+            rows_r.at[slot - 1],
+            dom=next_to[side],
+        )
+
+    row_copies = [pass_rows(send_rows, 1 + side, side) for side in range(2)]
+    near = [
+        [
+            pass_on(h, coarse.at[:, 256 * h : 256 * h + 256], 1 + side, side)
+            for side in range(2)
+        ]
+        for h in range(2)
     ]
-    to_left = [
-        remote(coarse, tiles.at[2], tile_s.at[1], tile_r.at[1], dom=chip(-1) * 2 + k),
-        remote(send_rows, rows.at[1], rows_s.at[1], rows_r.at[1], dom=chip(-1) * 2 + k),
-    ]
-    for copy in to_right + to_left:
+    for copy in row_copies + near[0] + near[1]:
         copy.start()
 
     lane = lax.broadcasted_iota(jnp.int32, (128, 128), 1).astype(F32)
@@ -153,21 +198,26 @@
 
     my_rows = pl.ds(pl.multiple_of(k * 128, 128), 128)
 
-    def at_home(table, tile, slot, rel):
-        sibbuf[slot] = picked(table, tile, me_d + other - k)
-        copy = remote(
-            sibbuf.at[slot],
-            recv.at[rel, my_rows],
-            sib_s.at[slot],
-            recv_sem.at[rel, k],
-            dom=c * 2 + other,
-        )
-        copy.start()
-        recv[rel, my_rows, :] = picked(table, tile, me_d)
-        return copy
-
-    loads[0].wait()
-    sib_copies = [at_home(send_rows, tiles.at[0], 0, 0)]
+    def at_home(table, slot, rel):
+        for h in range(2):
+            tile = tiles.at[h, slot]
+            lanes = slice(256 * h, 256 * h + 256)
+            sibbuf[h, slot] = picked(table, tile, me_d + other - k)
+            copy = remote(
+                sibbuf.at[h, slot],
+                recv.at[rel, my_rows, lanes],
+                sib_s.at[h, slot],
+                recv_sem.at[h, rel, k],
+                dom=c * 2 + other,
+            )
+            copy.start()
+            recv[rel, my_rows, lanes] = picked(table, tile, me_d)
+            sib_copies.append(copy)
+
+    sib_copies = []
+    for load in loads[:3]:
+        load.wait()
+    at_home(own_rows, 0, 0)
 
     def weights_of(t, carry):
         at = pl.ds(pl.multiple_of(t * 128, 128), 128)
@@ -197,8 +247,6 @@
         lax.fori_loop(0, 4, part, 0)
         return carry
 
-    lax.fori_loop(0, 16, weights_of, 0)
-
     def counts_of(t, carry):
         at = pl.ds(pl.multiple_of(t * 128, 128), 128)
         shift = ((t // 2) * 256).astype(F32)
@@ -221,56 +269,86 @@
         lax.fori_loop(0, 4, part, 0)
         return carry
 
+    for load in loads[3:8]:
+        load.wait()
     wht[...] = jnp.zeros((VP, 512), BF16)
     wht[:VARS, :] = w_head[...]
     kwp[...] = jnp.ones((8, 128), F32)
     kwp[0:1, :VARS] = kwidth[...]
     width = kwp[0:1, :]
     inv_b[...] = lanes_of(1.0 / (width * width))[:VP]
-    my_share = pl.ds(pl.multiple_of(me_m * 128, 128), 128)
     tgt[...] = jnp.zeros((VP, 128), F32)
-    tgt[:VARS, :] = targets[:, my_share].astype(F32)
+    tgt[:VARS, :] = targets[...].astype(F32)
 
     lax.fori_loop(0, 16, counts_of, 0)
 
-    for copy in to_right + to_left:
+    for copy in row_copies:
         copy.wait_recv()
-
-    def far_copy(side, j, o, kd):
+    row_copies += [pass_rows(rows.at[side], 3 + side, side) for side in range(2)]
+    for copy in row_copies[2:]:
+        copy.start()
+    next_one = []
+
+    def forward(h):
+        for side in range(2):
+            near[h][side].wait_recv()
+            copy = pass_on(h, tiles.at[h, 1 + side], 3 + side, side)
+            copy.start()
+            next_one.append(copy)
+
+    forward(0)
+    for load in loads[8:10]:
+        load.wait()
+    lax.fori_loop(0, 8, weights_of, 0)
+    forward(1)
+    at_home(rows.at[0], 1, 7)
+    at_home(rows.at[1], 2, 1)
+    lax.fori_loop(8, 16, weights_of, 0)
+    for load in loads[10:]:
+        load.wait()
+
+    def far_copy(h, side, j, o, kd):
         dest = chip(o) * 2 + kd
         rel = 4 + (j + 1) // 2 if side == 0 else 4 - (j + 1) // 2
         return dest, remote(
-            sbuf.at[side, j],
-            recv.at[rel, my_rows],
-            g_s.at[side, j],
-            recv_sem.at[rel, k],
+            sbuf.at[h, side, j],
+            recv.at[rel, my_rows, 256 * h : 256 * h + 256],
+            g_s.at[h, side, j],
+            recv_sem.at[h, rel, k],
             dom=dest,
         )
 
-    def both_ways(j, carry):
-        o = 3 - (j + 1) // 2
-        even = lax.rem(j, 2)
-        for side in range(2):
-            dest, copy = far_copy(side, j, o if side == 0 else -o, even if side == 0 else 1 - even)
-            sbuf[side, j] = picked(rows.at[side], tiles.at[1 + side], dest)
-            copy.start()
-        return carry
-
-    lax.fori_loop(0, 5, both_ways, 0)
-    sib_copies.append(at_home(rows.at[0], tiles.at[1], 1, 7))
-    sib_copies.append(at_home(rows.at[1], tiles.at[2], 2, 1))
-
-    loads[1].wait()
+    def send_far(h):
+        for copy in next_one[2 * h : 2 * h + 2]:
+            copy.wait_recv()
+
+        def both_ways(j, carry):
+            o = 2 - (j + 1) // 2
+            even = lax.rem(j, 2)
+            for side in range(2):
+                dest, copy = far_copy(
+                    h, side, j, o if side == 0 else -o, even if side == 0 else 1 - even
+                )
+                sbuf[h, side, j] = picked(rows.at[2 + side], tiles.at[h, 3 + side], dest)
+                copy.start()
+            return carry
+
+        lax.fori_loop(0, 3, both_ways, 0)
 
     def arrived(rel, kb):
         half = pl.ds(pl.multiple_of(kb * 128, 128), 128)
-        remote(
-            sibbuf.at[0], recv.at[rel, half], sib_s.at[0], recv_sem.at[rel, kb], dom=c * 2 + other
-        ).wait_recv()
+        for h in range(2):
+            remote(
+                sibbuf.at[h, 0],
+                recv.at[rel, half, 256 * h : 256 * h + 256],
+                sib_s.at[h, 0],
+                recv_sem.at[h, rel, kb],
+                dom=c * 2 + other,
+            ).wait_recv()
 
     def added(rels, t):
         at = pl.ds(pl.multiple_of(t * 512, 512), 512)
-        total = skipv[at, :].astype(F32) if rels == (0,) else acc[at, :]
+        total = skipv[at, :].astype(F32) if rels[0] == 0 else acc[at, :]
         for rel in rels:
             here = chip(rel)
             table = recv[rel]
@@ -278,10 +356,10 @@
             total = total + jnp.dot(wbuf[here, at, 256:], table, preferred_element_type=F32)
         return at, total
 
-    for rels in ((0,), (7, 1), (4,), (5, 3)):
+    def unpool(rels):
         for rel in rels:
             arrived(rel, other)
-            if rel not in (0, 7, 1):
+            if rel in (3, 4, 5):
                 arrived(rel, k)
 
         def accumulate(t, carry, rels=rels):
@@ -291,12 +369,22 @@
 
         lax.fori_loop(0, 4, accumulate, 0)
 
-    for rel in (6, 2):
+    for copy in row_copies[2:]:
+        copy.wait_recv()
+    send_far(0)
+    unpool((0,))
+    unpool((7, 1))
+    send_far(1)
+    at_home(rows.at[2], 3, 6)
+    at_home(rows.at[3], 4, 2)
+    unpool((6, 2))
+    unpool((4,))
+    for rel in (5, 3):
         arrived(rel, 0)
         arrived(rel, 1)
 
     def finish(t, carry):
-        total = added((6, 2), t)[1]
+        total = added((5, 3), t)[1]
         ext[pl.ds(pl.multiple_of(t * 512 + 128, 128), 512), :] = total.astype(BF16)
         return carry
 
@@ -320,8 +408,6 @@
     for rim in rims:
         rim.start()
     lax.fori_loop(1, 3, finish, 0)
-    loads[2].wait()
-    loads[3].wait()
 
     gain_row = gain[...]
 
@@ -392,7 +478,7 @@
 
     lax.fori_loop(0, 16, widen, 0)
     place = lax.broadcasted_iota(jnp.int32, (1, 128), 1) + me_m * 128
-    weight = jnp.broadcast_to(jnp.where(place < live[0], area[:, my_share], 0.0), (8, 128))
+    weight = jnp.broadcast_to(jnp.where(place < live[0], area[...], 0.0), (8, 128))
 
     def scores(q, carry):
         at = pl.ds(pl.multiple_of(q * 8, 8), 8)
@@ -413,29 +499,39 @@
             pf[i, at, :] = scale * (e * jnp.exp(e * e * halved) - total[i] * (1.0 / 16))
         return carry
 
-    lax.fori_loop(0, VP // 8, scores, 0)
-    gs[:, my_share] = pf[0].astype(BF16)
-
-    def gs_copy(r):
-        return remote(ssend.at[r], gs.at[:, my_share], gs_s.at[r], gs_r.at[r], mem=member(-r))
-
-    def give_back(r, carry):
-        ssend[r] = pf[r].astype(BF16)
-        gs_copy(r).start()
-        return carry
-
-    lax.fori_loop(1, 16, give_back, 0)
+
+    def gs_copy(v, r, share, back):
+        return remote(
+            ssend.at[r, pl.ds(48 * v, 48)],
+            gs.at[pl.ds(48 * v, 48), share],
+            gs_s.at[v, r],
+            gs_r.at[v, r],
+            mem=back,
+        )
+
+    for v in range(2):
+        lax.fori_loop(6 * v, 6 * v + 6, scores, 0)
+
+        def give_back(r, carry, v=v):
+            ssend[r, 48 * v : 48 * v + 48, :] = pf[r, 48 * v : 48 * v + 48, :].astype(BF16)
+            gs_copy(v, r, my_share, member(-r)).start()
+            return carry
+
+        lax.fori_loop(1, 16, give_back, 0)
+        gs[48 * v : 48 * v + 48, my_share] = pf[0, 48 * v : 48 * v + 48, :].astype(BF16)
 
     def gs_wait(r, carry):
         share = pl.ds(pl.multiple_of(member(r) * 128, 128), 128)
-        remote(ssend.at[r], gs.at[:, share], gs_s.at[r], gs_r.at[r], mem=member(r)).wait_recv()
+        for v in range(2):
+            gs_copy(v, r, share, member(r)).wait_recv()
         return carry
 
     lax.fori_loop(1, 16, gs_wait, 0)
 
     head = jnp.dot(gs[...], hidden[...], preferred_element_type=F32)
     for j in range(16):
-        hp[j] = head[24 * (j // 4) : 24 * (j // 4) + 24, 128 * (j % 4) : 128 * (j % 4) + 128]
+        lo, left = 24 * (j // 4), 128 * (j % 4)
+        hp[j] = head[lo : lo + 24, left : left + 128].astype(BF16)
 
     def hr_copy(r):
         return remote(hp.at[member(r)], hr.at[r], hr_s.at[r], hr_r.at[r], mem=member(r))
@@ -453,7 +549,7 @@
         return carry
 
     lax.fori_loop(0, 16, turn, 0)
-    turned = pltpu.make_async_copy(gst, gs_out, loc_sem.at[4])
+    turned = pltpu.make_async_copy(gst, gs_out, loc_sem.at[14])
     turned.start()
 
     def hr_wait(r, carry):
@@ -461,10 +557,10 @@
         return carry
 
     lax.fori_loop(1, 16, hr_wait, 0)
-    summed = hr[0]
+    summed = hr[0].astype(F32)
     for r in range(1, 16):
-        summed = summed + hr[r]
-    summed = summed * (1.0 / math.sqrt(32768))
+        summed = summed + hr[r].astype(F32)
+    summed = (summed * (1.0 / math.sqrt(32768))).astype(BF16)
     hs[...] = summed
     hall[me_m] = summed
 
@@ -485,26 +581,28 @@
     for j in range(16):
         lo = 24 * (j // 4)
         n = min(24, VARS - lo)
-        head_out[lo : lo + n, 0, 128 * (j % 4) : 128 * (j % 4) + 128] = hall[j, :n]
+        head_out[lo : lo + n, 0, 128 * (j % 4) : 128 * (j % 4) + 128] = hall[j].astype(F32)[:n]
 
     turned.wait()
-    for copy in to_right + to_left + sib_copies:
+    for copy in row_copies + near[0] + near[1] + next_one + sib_copies:
         copy.wait_send()
 
     def far_done(j, carry):
-        o = 3 - (j + 1) // 2
+        o = 2 - (j + 1) // 2
         even = lax.rem(j, 2)
-        for side in range(2):
-            far_copy(side, j, o if side == 0 else -o, even if side == 0 else 1 - even)[
-                1
-            ].wait_send()
-        return carry
-
-    lax.fori_loop(0, 5, far_done, 0)
+        for h in range(2):
+            for side in range(2):
+                far_copy(h, side, j, o if side == 0 else -o, even if side == 0 else 1 - even)[
+                    1
+                ].wait_send()
+        return carry
+
+    lax.fori_loop(0, 3, far_done, 0)
 
     def members_done(r, carry):
         pred_copy(member(r))[1].wait_send()
-        gs_copy(r).wait_send()
+        for v in range(2):
+            gs_copy(v, r, my_share, member(-r)).wait_send()
         hr_copy(r).wait_send()
         ha_copy(r, me_m).wait_send()
         return carry
@@ -539,17 +637,26 @@
             jax.ShapeDtypeStruct((2048, VARS), BF16),
             jax.ShapeDtypeStruct((VARS, 1, 512), F32),
         ),
-        in_specs=[hbm, vmem, vmem, vmem, vmem, smem, vmem, hbm, vmem, vmem, hbm, hbm, vmem, vmem],
+        in_specs=[hbm] * 5 + [smem] + [hbm] * 8,
         out_specs=(hbm, vmem),
         scratch_shapes=[
-            pltpu.VMEM((3, 512, 512), BF16),
-            pltpu.VMEM((2, 16, 128), jnp.int32),
+            pltpu.VMEM((16, 128), jnp.int32),
+            pltpu.VMEM((3, 2048), jnp.int32),
+            pltpu.VMEM((3, 2048), F32),
+            pltpu.VMEM((6, 2048), jnp.int32),
+            pltpu.VMEM((1, 128), F32),
+            pltpu.VMEM((VARS, 128), BF16),
+            pltpu.VMEM((1, VARS), F32),
+            pltpu.VMEM((1, 512), F32),
+            pltpu.VMEM((VARS, 512), BF16),
+            pltpu.VMEM((2, 5, 512, 256), BF16),
+            pltpu.VMEM((4, 16, 128), jnp.int32),
             pltpu.VMEM((8, 2048, 512), BF16),
             pltpu.VMEM((2048, 512), BF16),
             pltpu.VMEM((6, 128, 128), F32),
             pltpu.VMEM((8, 256, 512), BF16),
-            pltpu.VMEM((2, 5, 128, 512), BF16),
-            pltpu.VMEM((3, 128, 512), BF16),
+            pltpu.VMEM((2, 2, 3, 128, 256), BF16),
+            pltpu.VMEM((2, 5, 128, 256), BF16),
             pltpu.VMEM((2048, 512), F32),
             pltpu.VMEM((2048, 512), BF16),
             pltpu.VMEM((2304, 512), BF16),
@@ -566,24 +673,24 @@
             pltpu.VMEM((16, VP, 128), BF16),
             pltpu.VMEM((VP, 2048), BF16),
             pltpu.VMEM((2048, VARS), BF16),
-            pltpu.VMEM((16, 24, 128), F32),
-            pltpu.VMEM((16, 24, 128), F32),
-            pltpu.VMEM((24, 128), F32),
-            pltpu.VMEM((16, 24, 128), F32),
-            dma((5,)),
-            dma((2,)),
-            dma((2,)),
-            dma((2,)),
-            dma((2,)),
+            pltpu.VMEM((16, 24, 128), BF16),
+            pltpu.VMEM((16, 24, 128), BF16),
+            pltpu.VMEM((24, 128), BF16),
+            pltpu.VMEM((16, 24, 128), BF16),
+            dma((15,)),
+            dma((2, 4)),
+            dma((2, 4)),
+            dma((4,)),
+            dma((4,)),
+            dma((2, 2, 3)),
             dma((2, 5)),
-            dma((3,)),
-            dma((8, 2)),
+            dma((2, 8, 2)),
             dma((2,)),
             dma((2,)),
             dma((16,)),
             dma((16,)),
-            dma((16,)),
-            dma((16,)),
+            dma((2, 16)),
+            dma((2, 16)),
             dma((16,)),
             dma((16,)),
             dma((16,)),

time: 99.4 us -> 92.1 us (0.927); the launches traced: 97.9 us -> 92 us
  Pallas kernels: 92.8 us -> 86.9 us
    pallas_call x1, Pallas kernels: 92.8 us -> 86.9 us  [shards(): pl.pallas_call(kernel, name='decoder_tail', out_shape=(jax.ShapeDtypeStru...]
where the time goes in v4:
time: 92.1 us; the launch traced here: 92 us
  Pallas kernels  86.9 us (94%)
  matrix products  3.09 us (3%)
  between operations  1.31 us (1%)
    pallas_call x1, Pallas kernels, shards(): pl.pallas_call(kernel, name='decoder_tail', out_shape=(jax.ShapeDtypeStru...  86.9 us
    dot_general x1, matrix products, shards(): lax.dot_general(gscore, w_head, (((1,), (1,)), ((), ())), preferred_eleme...  3.09 us

profile of v4, /device:TPU:8, one launch (start us, length us, event | category | flops | bytes accessed | tf_op | source)
XLA Modules:
  0.0 92.0 jit_solution(14393237175781798162)
XLA Ops:
  1.3 0.0 copy-start
  1.3 86.9 %decoder_tail.1 = (bf16[2048,83]{1,0:T(8,128)(2,1)}, f32[83,1,512]{2,1,0:T(1,128)}) custom-call(bf16[512,512]{1,0:T(8,128)(2,1)} %bitcast.11, s32[16,128]{1,0:T(8,128)} %bitcast.14, s32[3,2048]{1,0:T(4,128)} %up_index_h.1, f32[3,2048]{1,0:T(4,128)} %up_weight_h.1, s32[6,2048]{1,0:T(8,128)} %neighbors_h.1, s32[1]{0:T(128)S(6)} %copy.17.live, ...), custom_call_target="tpu_custom_call" | custom-call | tf_op jit(solution)/shard_map/decoder_tail/pallas_call | solution.py:633
  88.2 0.0 copy-start.1
  88.2 0.0 copy-done
  88.2 3.1 %fusion = bf16[1,2048,512]{2,1,0:T(8,128)(2,1)} fusion(bf16[2048,83]{1,0:T(8,128)(2,1)} %get-tuple-element.4, bf16[512,83]{0,1:T(8,128)(2,1)S(1)} %copy-done), kind=kOutput, calls=%fused_computation.1 | convolution fusion | flops 175112192 | bytes 2522112 | tf_op jit(solution)/shard_map/dot_general | solution.py:718
  91.3 0.0 copy-done.1
  91.3 0.7 copy.18
Async XLA Ops:
  1.3 86.9 %copy-start = (bf16[512,83]{0,1:T(8,128)(2,1)S(1)}, bf16[512,83]{0,1:T(8,128)(2,1)}, u32[]{:S(2)}) copy-start(bf16[512,83]{0,1:T(8,128)(2,1)} %param.27) | copy-start | bytes 254980
  88.2 3.1 %copy-start.1 = (f32[83,1,512]{2,1,0:T(1,128)S(1)}, f32[83,1,512]{2,1,0:T(1,128)}, u32[]{:S(2)}) copy-start(f32[83,1,512]{2,1,0:T(1,128)} %get-tuple-element.5) | copy-start | bytes 509956

commit v5 on v4

--- a/solution.py
+++ b/solution.py
@@ -34,7 +34,7 @@
     w_out,
     gain_h,
     w_head_h,
-    gs_out,
+    grad_out,
     head_out,
     own_rows,
     up_index,
@@ -68,12 +68,12 @@
     pf,
     ssend,
     gs,
-    gst,
     hp,
     hr,
     hs,
     hall,
     loc_sem,
+    grad_sem,
     tile_s,
     tile_r,
     rows_s,
@@ -510,7 +510,7 @@
         )
 
     for v in range(2):
-        lax.fori_loop(6 * v, 6 * v + 6, scores, 0)
+        lax.fori_loop(6 * v, min(6 * v + 6, -(-VARS // 8)), scores, 0)
 
         def give_back(r, carry, v=v):
             ssend[r, 48 * v : 48 * v + 48, :] = pf[r, 48 * v : 48 * v + 48, :].astype(BF16)
@@ -543,14 +543,19 @@
     lax.fori_loop(1, 16, spread, 0)
     hr[0] = hp[me_m]
 
-    def turn(j, carry):
-        at = pl.ds(pl.multiple_of(j * 128, 128), 128)
-        gst[at, :] = gs[:, at].astype(F32).T[:, :VARS].astype(BF16)
-        return carry
-
-    lax.fori_loop(0, 16, turn, 0)
-    turned = pltpu.make_async_copy(gst, gs_out, loc_sem.at[14])
-    turned.start()
+    def grad_copy(j):
+        at = pl.ds(pl.multiple_of(j * 512, 512), 512)
+        return pltpu.make_async_copy(skipv.at[at], grad_out.at[at], grad_sem.at[j])
+
+    def gradient(j, carry):
+        at = pl.ds(pl.multiple_of(j * 512, 512), 512)
+        skipv[at, :] = lax.dot_general(
+            gs[:, at], wht[...], (((0,), (0,)), ((), ())), preferred_element_type=F32
+        ).astype(BF16)
+        grad_copy(j).start()
+        return carry
+
+    lax.fori_loop(0, 4, gradient, 0)
 
     def hr_wait(r, carry):
         hr_copy(r).wait_recv()
@@ -573,17 +578,6 @@
 
     lax.fori_loop(1, 16, tell, 0)
 
-    def ha_wait(r, carry):
-        ha_copy(r, member(-r)).wait_recv()
-        return carry
-
-    lax.fori_loop(1, 16, ha_wait, 0)
-    for j in range(16):
-        lo = 24 * (j // 4)
-        n = min(24, VARS - lo)
-        head_out[lo : lo + n, 0, 128 * (j % 4) : 128 * (j % 4) + 128] = hall[j].astype(F32)[:n]
-
-    turned.wait()
     for copy in row_copies + near[0] + near[1] + next_one + sib_copies:
         copy.wait_send()
 
@@ -604,10 +598,32 @@
         for v in range(2):
             gs_copy(v, r, my_share, member(-r)).wait_send()
         hr_copy(r).wait_send()
+        return carry
+
+    lax.fori_loop(1, 16, members_done, 0)
+
+    def grad_done(j, carry):
+        grad_copy(j).wait()
+        return carry
+
+    lax.fori_loop(0, 4, grad_done, 0)
+
+    def ha_wait(r, carry):
+        ha_copy(r, member(-r)).wait_recv()
+        return carry
+
+    lax.fori_loop(1, 16, ha_wait, 0)
+    for j in range(16):
+        lo = 24 * (j // 4)
+        n = min(24, VARS - lo)
+        head_out[lo : lo + n, 0, 128 * (j % 4) : 128 * (j % 4) + 128] = hall[j].astype(F32)[:n]
+
+
+    def told(r, carry):
         ha_copy(r, me_m).wait_send()
         return carry
 
-    lax.fori_loop(1, 16, members_done, 0)
+    lax.fori_loop(1, 16, told, 0)
 
 
 def shards(
@@ -630,11 +646,11 @@
     vmem = pl.BlockSpec(memory_space=pltpu.VMEM)
     smem = pl.BlockSpec(memory_space=pltpu.SMEM)
     dma = pltpu.SemaphoreType.DMA
-    gscore, head = pl.pallas_call(
+    grad_latent, head = pl.pallas_call(
         kernel,
         name="decoder_tail",
         out_shape=(
-            jax.ShapeDtypeStruct((2048, VARS), BF16),
+            jax.ShapeDtypeStruct((2048, 512), BF16),
             jax.ShapeDtypeStruct((VARS, 1, 512), F32),
         ),
         in_specs=[hbm] * 5 + [smem] + [hbm] * 8,
@@ -672,12 +688,12 @@
             pltpu.VMEM((16, VP, 128), F32),
             pltpu.VMEM((16, VP, 128), BF16),
             pltpu.VMEM((VP, 2048), BF16),
-            pltpu.VMEM((2048, VARS), BF16),
             pltpu.VMEM((16, 24, 128), BF16),
             pltpu.VMEM((16, 24, 128), BF16),
             pltpu.VMEM((24, 128), BF16),
             pltpu.VMEM((16, 24, 128), BF16),
-            dma((15,)),
+            dma((14,)),
+            dma((4,)),
             dma((2, 4)),
             dma((2, 4)),
             dma((4,)),
@@ -715,9 +731,6 @@
         ln_gain[None],
         w_head.T,
     )
-    grad_latent = lax.dot_general(
-        gscore, w_head, (((1,), (1,)), ((), ())), preferred_element_type=F32
-    ).astype(BF16)
     return grad_latent[None], head.transpose(1, 2, 0)
 
 

time: 92.1 us -> 91.8 us (level)
  matrix products: 3.09 us -> 0 us
  local copies, waits for them, and re-layouts: 0.68 us -> 3.76 us
    dot_general x1 -> x0, matrix products: 3.09 us -> none  [shards(): lax.dot_general(gscore, w_head, (((1,), (1,)), ((), ())), preferred_eleme...]
    unnamed x5 -> x4, local copies, waits for them, and re-layouts: 0.68 us -> 3.76 us
where the time goes in v5:
time: 91.8 us; the launch traced here: 91.7 us
  Pallas kernels  86.6 us (94%)
  local copies, waits for them, and re-layouts  3.76 us (4%)
  between operations  1.3 us (1%)
    pallas_call x1, Pallas kernels, shards(): pl.pallas_call(kernel, name='decoder_tail', out_shape=(jax.ShapeDtypeStru...  86.6 us
    unnamed x4, local copies, waits for them, and re-layouts  3.76 us

profile of v5, /device:TPU:8, one launch (start us, length us, event | category | flops | bytes accessed | tf_op | source)
XLA Modules:
  0.0 91.7 jit_solution(3414282460434097944)
XLA Ops:
  1.3 86.6 %decoder_tail.1 = (bf16[2048,512]{1,0:T(8,128)(2,1)}, f32[83,1,512]{2,1,0:T(1,128)}) custom-call(bf16[512,512]{1,0:T(8,128)(2,1)} %bitcast.9, s32[16,128]{1,0:T(8,128)} %bitcast.12, s32[3,2048]{1,0:T(4,128)} %up_index_h.1, f32[3,2048]{1,0:T(4,128)} %up_weight_h.1, s32[6,2048]{1,0:T(8,128)} %neighbors_h.1, s32[1]{0:T(128)S(6)} %copy.18.live, ...), custom_call_target="tpu_custom_call" | custom-call | tf_op jit(solution)/shard_map/decoder_tail/pallas_call | solution.py:649
  87.9 0.0 copy-start
  87.9 3.1 %copy.19 = bf16[1,2048,512]{2,1,0:T(8,128)(2,1)} copy(bf16[1,2048,512]{2,1,0:T(8,128)(2,1)} %bitcast.8) | data formatting | bytes 4194304
  91.0 0.0 copy-done
  91.0 0.7 copy.20
Async XLA Ops:
  87.9 3.1 %copy-start = (f32[83,1,512]{2,1,0:T(1,128)S(1)}, f32[83,1,512]{2,1,0:T(1,128)}, u32[]{:S(2)}) copy-start(f32[83,1,512]{2,1,0:T(1,128)} %get-tuple-element.5) | copy-start | bytes 509956

commit v6 on v5

--- a/solution.py
+++ b/solution.py
@@ -151,8 +151,6 @@
             )
         )
     ]
-    for load in loads:
-        load.start()
     pl.semaphore_wait(barrier, 30)
 
     next_to = (chip(1) * 2 + k, chip(-1) * 2 + k)
@@ -185,6 +183,8 @@
     ]
     for copy in row_copies + near[0] + near[1]:
         copy.start()
+    for load in loads:
+        load.start()
 
     lane = lax.broadcasted_iota(jnp.int32, (128, 128), 1).astype(F32)
 
@@ -309,7 +309,7 @@
 
     def far_copy(h, side, j, o, kd):
         dest = chip(o) * 2 + kd
-        rel = 4 + (j + 1) // 2 if side == 0 else 4 - (j + 1) // 2
+        rel = 5 - j // 2 if side == 0 else 3 + j // 2
         return dest, remote(
             sbuf.at[h, side, j],
             recv.at[rel, my_rows, 256 * h : 256 * h + 256],
@@ -323,7 +323,7 @@
             copy.wait_recv()
 
         def both_ways(j, carry):
-            o = 2 - (j + 1) // 2
+            o = 1 + j // 2
             even = lax.rem(j, 2)
             for side in range(2):
                 dest, copy = far_copy(
@@ -378,13 +378,12 @@
     at_home(rows.at[2], 3, 6)
     at_home(rows.at[3], 4, 2)
     unpool((6, 2))
-    unpool((4,))
-    for rel in (5, 3):
-        arrived(rel, 0)
-        arrived(rel, 1)
+    unpool((5, 3))
+    arrived(4, 0)
+    arrived(4, 1)
 
     def finish(t, carry):
-        total = added((5, 3), t)[1]
+        total = added((4,), t)[1]
         ext[pl.ds(pl.multiple_of(t * 512 + 128, 128), 512), :] = total.astype(BF16)
         return carry
 
@@ -582,7 +581,7 @@
         copy.wait_send()
 
     def far_done(j, carry):
-        o = 2 - (j + 1) // 2
+        o = 1 + j // 2
         even = lax.rem(j, 2)
         for h in range(2):
             for side in range(2):

time: 91.8 us -> 91.2 us (level)
    pallas_call x1, Pallas kernels: 86.6 us -> 85.7 us  [shards(): pl.pallas_call(kernel, name='decoder_tail', out_shape=(jax.ShapeDtypeStru...]
where the time goes in v6:
time: 91.2 us; the launch traced here: 90.7 us
  Pallas kernels  85.7 us (94%)
  local copies, waits for them, and re-layouts  3.76 us (4%)
  between operations  1.3 us (1%)
    pallas_call x1, Pallas kernels, shards(): pl.pallas_call(kernel, name='decoder_tail', out_shape=(jax.ShapeDtypeStru...  85.7 us
    unnamed x4, local copies, waits for them, and re-layouts  3.76 us

profile of v6, /device:TPU:8, one launch (start us, length us, event | category | flops | bytes accessed | tf_op | source)
XLA Modules:
  0.0 90.7 jit_solution(10962908669705082845)
XLA Ops:
  1.3 85.7 %decoder_tail.1 = (bf16[2048,512]{1,0:T(8,128)(2,1)}, f32[83,1,512]{2,1,0:T(1,128)}) custom-call(bf16[512,512]{1,0:T(8,128)(2,1)} %bitcast.9, s32[16,128]{1,0:T(8,128)} %bitcast.12, s32[3,2048]{1,0:T(4,128)} %up_index_h.1, f32[3,2048]{1,0:T(4,128)} %up_weight_h.1, s32[6,2048]{1,0:T(8,128)} %neighbors_h.1, s32[1]{0:T(128)S(6)} %copy.18.live, ...), custom_call_target="tpu_custom_call" | custom-call | tf_op jit(solution)/shard_map/decoder_tail/pallas_call | solution.py:648
  87.0 0.0 copy-start
  87.0 3.1 %copy.19 = bf16[1,2048,512]{2,1,0:T(8,128)(2,1)} copy(bf16[1,2048,512]{2,1,0:T(8,128)(2,1)} %bitcast.8) | data formatting | bytes 4194304
  90.1 0.0 copy-done
  90.1 0.7 copy.20
Async XLA Ops:
  87.0 3.1 %copy-start = (f32[83,1,512]{2,1,0:T(1,128)S(1)}, f32[83,1,512]{2,1,0:T(1,128)}, u32[]{:S(2)}) copy-start(f32[83,1,512]{2,1,0:T(1,128)} %get-tuple-element.5) | copy-start | bytes 509956

commit v7 on v6

--- a/solution.py
+++ b/solution.py
@@ -72,6 +72,7 @@
     hr,
     hs,
     hall,
+    word,
     loc_sem,
     grad_sem,
     tile_s,
@@ -116,19 +117,27 @@
 
     barrier = pltpu.get_barrier_semaphore()
 
-    def greet(r, carry):
-        pl.semaphore_signal(
-            barrier,
-            inc=1,
-            device_id={"dom": lax.rem(me_d + r, 16)},
-            device_id_type=pl.DeviceIdType.MESH,
-        )
-        pl.semaphore_signal(
-            barrier, inc=1, device_id={"mem": member(r)}, device_id_type=pl.DeviceIdType.MESH
-        )
-        return carry
-
-    lax.fori_loop(1, 16, greet, 0)
+    east = lax.rem(me_m, 4)
+    north = me_m // 4
+    z_ring = [{"dom": chip(step) * 2 + k} for step in (1, -1)]
+    x_ring = [{"mem": north * 4 + lax.rem(east + step, 4)} for step in (1, 3)]
+    y_ring = [{"mem": lax.rem(north + step, 4) * 4 + east} for step in (1, 3)]
+    pair = [{"dom": c * 2 + other}]
+
+    def greet(sem, devices):
+        for device in devices:
+            pl.semaphore_signal(
+                sem, inc=1, device_id=device, device_id_type=pl.DeviceIdType.MESH
+            )
+
+    rounds = (z_ring, z_ring, z_ring, pair, x_ring, y_ring, y_ring)
+
+    def heard(i):
+        pl.semaphore_wait(word.at[i], len(rounds[i]))
+        if i + 1 < len(rounds):
+            greet(word.at[i + 1], rounds[i + 1])
+
+    greet(barrier, z_ring + pair + x_ring + y_ring)
     my_share = pl.ds(pl.multiple_of(me_m * 128, 128), 128)
     loads = [
         pltpu.make_async_copy(src, dst, loc_sem.at[i])
@@ -151,7 +160,7 @@
             )
         )
     ]
-    pl.semaphore_wait(barrier, 30)
+    pl.semaphore_wait(barrier, 7)
 
     next_to = (chip(1) * 2 + k, chip(-1) * 2 + k)
 
@@ -183,6 +192,7 @@
     ]
     for copy in row_copies + near[0] + near[1]:
         copy.start()
+    greet(word.at[0], rounds[0])
     for load in loads:
         load.start()
 
@@ -218,6 +228,7 @@
     for load in loads[:3]:
         load.wait()
     at_home(own_rows, 0, 0)
+    heard(0)
 
     def weights_of(t, carry):
         at = pl.ds(pl.multiple_of(t * 128, 128), 128)
@@ -280,7 +291,9 @@
     tgt[...] = jnp.zeros((VP, 128), F32)
     tgt[:VARS, :] = targets[...].astype(F32)
 
+    heard(1)
     lax.fori_loop(0, 16, counts_of, 0)
+    heard(2)
 
     for copy in row_copies:
         copy.wait_recv()
@@ -300,10 +313,14 @@
     for load in loads[8:10]:
         load.wait()
     lax.fori_loop(0, 8, weights_of, 0)
+    heard(3)
+    heard(4)
     forward(1)
     at_home(rows.at[0], 1, 7)
     at_home(rows.at[1], 2, 1)
     lax.fori_loop(8, 16, weights_of, 0)
+    heard(5)
+    heard(6)
     for load in loads[10:]:
         load.wait()
 
@@ -691,6 +708,7 @@
             pltpu.VMEM((16, 24, 128), BF16),
             pltpu.VMEM((24, 128), BF16),
             pltpu.VMEM((16, 24, 128), BF16),
+            pltpu.SemaphoreType.REGULAR((7,)),
             dma((14,)),
             dma((4,)),
             dma((2, 4)),

time: 91.2 us -> 93.5 us (1.025)
  Pallas kernels: 85.7 us -> 88.1 us
    pallas_call x1, Pallas kernels: 85.7 us -> 88.1 us  [shards(): pl.pallas_call(kernel, name='decoder_tail', out_shape=(jax.ShapeDtypeStru...]
where the time goes in v7:
time: 93.5 us; the launch traced here: 93.2 us
  Pallas kernels  88.1 us (94%)
  local copies, waits for them, and re-layouts  3.76 us (4%)
  between operations  1.3 us (1%)
    pallas_call x1, Pallas kernels, shards(): pl.pallas_call(kernel, name='decoder_tail', out_shape=(jax.ShapeDtypeStru...  88.1 us
    unnamed x4, local copies, waits for them, and re-layouts  3.76 us

profile of v7, /device:TPU:8, one launch (start us, length us, event | category | flops | bytes accessed | tf_op | source)
XLA Modules:
  0.0 93.2 jit_solution(18316393311875645037)
XLA Ops:
  1.3 88.1 %decoder_tail.1 = (bf16[2048,512]{1,0:T(8,128)(2,1)}, f32[83,1,512]{2,1,0:T(1,128)}) custom-call(bf16[512,512]{1,0:T(8,128)(2,1)} %bitcast.9, s32[16,128]{1,0:T(8,128)} %bitcast.12, s32[3,2048]{1,0:T(4,128)} %up_index_h.1, f32[3,2048]{1,0:T(4,128)} %up_weight_h.1, s32[6,2048]{1,0:T(8,128)} %neighbors_h.1, s32[1]{0:T(128)S(6)} %copy.18.live, ...), custom_call_target="tpu_custom_call" | custom-call | tf_op jit(solution)/shard_map/decoder_tail/pallas_call | solution.py:665
  89.4 0.0 copy-start
  89.4 3.1 %copy.19 = bf16[1,2048,512]{2,1,0:T(8,128)(2,1)} copy(bf16[1,2048,512]{2,1,0:T(8,128)(2,1)} %bitcast.8) | data formatting | bytes 4194304
  92.5 0.0 copy-done
  92.5 0.7 copy.20
Async XLA Ops:
  89.4 3.1 %copy-start = (f32[83,1,512]{2,1,0:T(1,128)S(1)}, f32[83,1,512]{2,1,0:T(1,128)}, u32[]{:S(2)}) copy-start(f32[83,1,512]{2,1,0:T(1,128)} %get-tuple-element.5) | copy-start | bytes 509956

commit v8 on v6

--- a/solution.py
+++ b/solution.py
@@ -430,24 +430,29 @@
         half = 0.5 * pre
         act = (half + half * jnp.tanh(half)).astype(BF16)
         upd = jnp.dot(act, wout[...], preferred_element_type=F32)
-        mean = jnp.sum(upd, axis=1, keepdims=True) * (1.0 / 512)
-        centred = upd - mean
-        var = jnp.sum(centred * centred, axis=1, keepdims=True) * (1.0 / 512)
-        h = (x.astype(F32) + centred * lax.rsqrt(var + 1e-05) * gain_row).astype(BF16)
-        hidden[pl.ds(pl.multiple_of(i * 512, 512), 512), :] = h
-        pred = lax.dot_general(wht[...], h, NT, preferred_element_type=F32).astype(BF16)
-        for s in range(4):
-            j = 4 * i + s
-            r, copy = pred_copy(j)
-            psend[j] = pred[:, s * 128 : s * 128 + 128]
-
-            @pl.when(r != 0)
-            def _():
-                copy.start()
-
-            @pl.when(r == 0)
-            def _():
-                pall[0] = psend[j]
+        for g in range(2):
+            u = upd[256 * g : 256 * g + 256]
+            mean = jnp.sum(u, axis=1, keepdims=True) * (1.0 / 512)
+            centred = u - mean
+            var = jnp.sum(centred * centred, axis=1, keepdims=True) * (1.0 / 512)
+            h = (
+                x[256 * g : 256 * g + 256].astype(F32)
+                + centred * lax.rsqrt(var + 1e-05) * gain_row
+            ).astype(BF16)
+            hidden[pl.ds(pl.multiple_of(i * 512 + 256 * g, 256), 256), :] = h
+            pred = lax.dot_general(wht[...], h, NT, preferred_element_type=F32).astype(BF16)
+            for s in range(2):
+                j = 4 * i + 2 * g + s
+                r, copy = pred_copy(j)
+                psend[j] = pred[:, s * 128 : s * 128 + 128]
+
+                @pl.when(r != 0)
+                def _():
+                    copy.start()
+
+                @pl.when(r == 0)
+                def _():
+                    pall[0] = psend[j]
 
         return carry
 
@@ -501,27 +506,27 @@
 
     def gs_copy(v, r, share, back):
         return remote(
-            ssend.at[r, pl.ds(48 * v, 48)],
-            gs.at[pl.ds(48 * v, 48), share],
+            ssend.at[r, pl.ds(32 * v, 32)],
+            gs.at[pl.ds(32 * v, 32), share],
             gs_s.at[v, r],
             gs_r.at[v, r],
             mem=back,
         )
 
-    for v in range(2):
-        lax.fori_loop(6 * v, min(6 * v + 6, -(-VARS // 8)), scores, 0)
+    for v in range(3):
+        lax.fori_loop(4 * v, min(4 * v + 4, -(-VARS // 8)), scores, 0)
 
         def give_back(r, carry, v=v):
-            ssend[r, 48 * v : 48 * v + 48, :] = pf[r, 48 * v : 48 * v + 48, :].astype(BF16)
+            ssend[r, 32 * v : 32 * v + 32, :] = pf[r, 32 * v : 32 * v + 32, :].astype(BF16)
             gs_copy(v, r, my_share, member(-r)).start()
             return carry
 
         lax.fori_loop(1, 16, give_back, 0)
-        gs[48 * v : 48 * v + 48, my_share] = pf[0, 48 * v : 48 * v + 48, :].astype(BF16)
+        gs[32 * v : 32 * v + 32, my_share] = pf[0, 32 * v : 32 * v + 32, :].astype(BF16)
 
     def gs_wait(r, carry):
         share = pl.ds(pl.multiple_of(member(r) * 128, 128), 128)
-        for v in range(2):
+        for v in range(3):
             gs_copy(v, r, share, member(r)).wait_recv()
         return carry
 
@@ -594,7 +599,7 @@
 
     def members_done(r, carry):
         pred_copy(member(r))[1].wait_send()
-        for v in range(2):
+        for v in range(3):
             gs_copy(v, r, my_share, member(-r)).wait_send()
         hr_copy(r).wait_send()
         return carry
@@ -704,8 +709,8 @@
             dma((2,)),
             dma((16,)),
             dma((16,)),
-            dma((2, 16)),
-            dma((2, 16)),
+            dma((3, 16)),
+            dma((3, 16)),
             dma((16,)),
             dma((16,)),
             dma((16,)),

time: 91.2 us -> 93.3 us (1.023)
  Pallas kernels: 85.7 us -> 87.7 us
    pallas_call x1, Pallas kernels: 85.7 us -> 87.7 us  [shards(): pl.pallas_call(kernel, name='decoder_tail', out_shape=(jax.ShapeDtypeStru...]
where the time goes in v8:
time: 93.3 us; the launch traced here: 92.8 us
  Pallas kernels  87.7 us (94%)
  local copies, waits for them, and re-layouts  3.76 us (4%)
  between operations  1.3 us (1%)
    pallas_call x1, Pallas kernels, shards(): pl.pallas_call(kernel, name='decoder_tail', out_shape=(jax.ShapeDtypeStru...  87.7 us
    unnamed x4, local copies, waits for them, and re-layouts  3.76 us

profile of v8, /device:TPU:8, one launch (start us, length us, event | category | flops | bytes accessed | tf_op | source)
XLA Modules:
  0.0 92.8 jit_solution(9349730628909058105)
XLA Ops:
  1.3 87.7 %decoder_tail.1 = (bf16[2048,512]{1,0:T(8,128)(2,1)}, f32[83,1,512]{2,1,0:T(1,128)}) custom-call(bf16[512,512]{1,0:T(8,128)(2,1)} %bitcast.9, s32[16,128]{1,0:T(8,128)} %bitcast.12, s32[3,2048]{1,0:T(4,128)} %up_index_h.1, f32[3,2048]{1,0:T(4,128)} %up_weight_h.1, s32[6,2048]{1,0:T(8,128)} %neighbors_h.1, s32[1]{0:T(128)S(6)} %copy.18.live, ...), custom_call_target="tpu_custom_call" | custom-call | tf_op jit(solution)/shard_map/decoder_tail/pallas_call | solution.py:653
  89.0 0.0 copy-start
  89.0 3.1 %copy.19 = bf16[1,2048,512]{2,1,0:T(8,128)(2,1)} copy(bf16[1,2048,512]{2,1,0:T(8,128)(2,1)} %bitcast.8) | data formatting | bytes 4194304
  92.1 0.0 copy-done
  92.1 0.7 copy.20
Async XLA Ops:
  89.0 3.1 %copy-start = (f32[83,1,512]{2,1,0:T(1,128)S(1)}, f32[83,1,512]{2,1,0:T(1,128)}, u32[]{:S(2)}) copy-start(f32[83,1,512]{2,1,0:T(1,128)} %get-tuple-element.5) | copy-start | bytes 509956
